TPU v7x, 32 devices: a whole 2x2x4 slice. The times are simulated.
32 devices in a mesh: seg: 4 (over y, x), gx: 2 (over core), gy: 4 (over z).
Axes of the slice: x: 2, y: 2, z: 4, core: 2. Of those that a mesh axis runs over, the one named last changes fastest.
Arguments:
- gas_state: float32 [7, 384, 32, 512], P(None, 'seg', 'gx', 'gy'), may hold values from 0 to 1
- solids_temp: float32 [384, 32, 512], P('seg', 'gx', 'gy'), may hold values from 0.2 to 1.2
- exchange_rate: float32 [32, 512], P('gx', 'gy'), may hold values from 0.1 to 0.5
- column_flags: int32 [32, 512], P('gx', 'gy'), may hold values from 0 to 3
- block_inverse: float32 [384, 96], P('seg'), may hold values from -1 to 2, as said below
- line_coupling: float32 [4, 2], P('seg'), may hold values from 0.05 to 0.25
Outputs:
- gas_next: float32 [7, 384, 32, 512], P(None, 'seg', 'gx', 'gy')
- solids_next: float32 [384, 32, 512], P('seg', 'gx', 'gy')
Inputs may be any that keep to these rules, and one draw needn't show every extreme that they name: `block_inverse`: each block of 96 rows holds the inverse of that segment's diagonal block.
All inputs are finite; a program needn't handle non-finite values.
Results may differ from a plain program's by a relative error of at most 0.000061.
Values sent between devices are 32-bit elements; how exact they have to be, the bound alone decides.
A program may use at most 192 MiB of HBM per device.

v0:
```python
import jax
import jax.numpy as jnp
from jax import lax
from jax.sharding import PartitionSpec as P

diffusion = (0.1, 0.08, 0.12, 0.09, 0.11, 0.07)
stoich = (-1.0, -0.5, 1.0, 0.5, 0.25, 0.75)
rate_const = 0.3
upwind = 0.25
cond_base = 0.04
cond_slope = 0.3
heat_release = 0.5
lateral = 0.1
loss_table = (0.0, 0.3, 0.0, 0.1)
feed_table = (0.0, 0.0, 0.4, 0.0)
highest = lax.Precision.HIGHEST


def with_halo(block, sides, width):
    for axis, dim in sides:
        count = lax.axis_size(axis)
        forward = [(i, i + 1) for i in range(count - 1)]
        backward = [(target, source) for source, target in forward]
        low = lax.ppermute(
            lax.slice_in_dim(block, block.shape[dim] - width, None, axis=dim), axis, forward
        )
        high = lax.ppermute(lax.slice_in_dim(block, 0, width, axis=dim), axis, backward)
        block = jnp.concatenate([low, block, high], axis=dim)
    return block


def advance_species(padded, spread, gains, reaction):
    center = padded[:, 1:-1, 1:-1, 1:-1]
    beside = padded[:, 2:, 1:-1, 1:-1] + padded[:, :-2, 1:-1, 1:-1]
    beside = beside + padded[:, 1:-1, 2:, 1:-1] + padded[:, 1:-1, :-2, 1:-1]
    beside = beside + padded[:, 1:-1, 1:-1, 2:] + padded[:, 1:-1, 1:-1, :-2]
    below = padded[:, :-2, 1:-1, 1:-1]
    return (
        center
        + spread * (beside - 6.0 * center)
        - upwind * (center - below)
        + gains * reaction[None]
    )


def lookup(flags, table):
    result = jnp.zeros(flags.shape, jnp.float32)
    for value, entry in enumerate(table):
        result = result + jnp.where(flags == value, entry, 0.0)
    return result


def advance_enthalpy(heat_pad, mix_pad, reaction, flags):
    cond = cond_base + cond_slope * mix_pad
    heat_mid = heat_pad[1:-1, 1:-1, 1:-1]
    cond_mid = cond[1:-1, 1:-1, 1:-1]
    flux = jnp.zeros(heat_mid.shape, heat_mid.dtype)
    views = (
        (slice(2, None), slice(1, -1), slice(1, -1)),
        (slice(None, -2), slice(1, -1), slice(1, -1)),
        (slice(1, -1), slice(2, None), slice(1, -1)),
        (slice(1, -1), slice(None, -2), slice(1, -1)),
        (slice(1, -1), slice(1, -1), slice(2, None)),
        (slice(1, -1), slice(1, -1), slice(None, -2)),
    )
    for view in views:
        flux = flux + 0.5 * (cond_mid + cond[view]) * (heat_pad[view] - heat_mid)
    loss = lookup(flags, loss_table)[None]
    feed = lookup(flags, feed_table)[None]
    return heat_mid + flux + heat_release * reaction - loss * heat_mid + feed


def solid_source(temp_pad, temp, heat_new, exchange):
    beside = (
        temp_pad[:, 2:, 1:-1]
        + temp_pad[:, :-2, 1:-1]
        + temp_pad[:, 1:-1, 2:]
        + temp_pad[:, 1:-1, :-2]
    )
    return temp + lateral * (beside - 4.0 * temp) + exchange[None] * (heat_new - temp)


def reduced_inverse(scalars):
    count = scalars.shape[0]
    size = 2 * count
    index = jnp.arange(size)
    segment = index // 2
    odd = index % 2
    rows = scalars[segment]
    first = jnp.where(odd == 0, rows[:, 0], rows[:, 1]) * rows[:, 4]
    last = jnp.where(odd == 0, rows[:, 2], rows[:, 3]) * rows[:, 5]
    cols = index[None, :]
    matrix = jnp.eye(size, dtype=scalars.dtype)
    matrix = matrix - jnp.where(cols == (2 * segment - 1)[:, None], first[:, None], 0.0)
    matrix = matrix - jnp.where(cols == (2 * segment + 2)[:, None], last[:, None], 0.0)
    inverse = jnp.eye(size, dtype=scalars.dtype)
    for step in range(size):
        pivot_row = matrix[step] / matrix[step, step]
        pivot_inv = inverse[step] / matrix[step, step]
        is_pivot = index == step
        matrix = jnp.where(is_pivot[:, None], pivot_row[None], matrix)
        inverse = jnp.where(is_pivot[:, None], pivot_inv[None], inverse)
        factor = jnp.where(is_pivot, 0.0, matrix[:, step])
        matrix = matrix - factor[:, None] * pivot_row[None]
        inverse = inverse - factor[:, None] * pivot_inv[None]
    return inverse


def body(gas_state, solids_temp, exchange_rate, column_flags, block_inverse, line_coupling):
    species_count = gas_state.shape[0] - 1
    depth, width_x, width_y = solids_temp.shape
    spread = jnp.array(diffusion, jnp.float32)[:, None, None, None]
    gains = jnp.array(stoich, jnp.float32)[:, None, None, None]
    reaction = rate_const * gas_state[0] * gas_state[1]
    temp_pad = with_halo(solids_temp, (("gx", 1), ("gy", 2)), 1)
    padded = with_halo(gas_state, (("seg", 1), ("gx", 2), ("gy", 3)), 1)
    species_new = advance_species(padded[:species_count], spread, gains, reaction)
    mix = 0.5 * jnp.sum(species_new, axis=0)
    mix_pad = with_halo(mix, (("seg", 0), ("gx", 1), ("gy", 2)), 1)
    heat_pad = padded[species_count]
    heat_new = advance_enthalpy(heat_pad, mix_pad, reaction, column_flags)
    gas_next = jnp.concatenate([species_new, heat_new[None]], axis=0)
    source = solid_source(temp_pad, solids_temp, heat_new, exchange_rate)
    local = jnp.dot(block_inverse, source.reshape(depth, width_x * width_y), precision=highest)
    ends = jnp.stack([local[0], local[depth - 1]])
    scalars = jnp.stack(
        [
            block_inverse[0, 0],
            block_inverse[depth - 1, 0],
            block_inverse[0, depth - 1],
            block_inverse[depth - 1, depth - 1],
            line_coupling[0, 0],
            line_coupling[0, 1],
        ]
    )[None]
    segment_id = lax.axis_index("seg")
    all_ends, all_scalars = (
        lax.all_gather(ends, "seg", axis=0, tiled=True),
        lax.all_gather(scalars, "seg", axis=0, tiled=True),
    )
    inverse = reduced_inverse(all_scalars)
    index = jnp.arange(inverse.shape[0])
    select = jnp.stack([index == 2 * segment_id - 1, index == 2 * segment_id + 2]).astype(
        jnp.float32
    )
    picked = jnp.dot(select, inverse, precision=highest)
    near = jnp.dot(picked, all_ends, precision=highest)
    solved = local + line_coupling[0, 0] * near[0][None, :] * block_inverse[:, 0:1]
    solved = solved + line_coupling[0, 1] * near[1][None, :] * block_inverse[:, depth - 1 : depth]
    return (gas_next, solved.reshape(depth, width_x, width_y))


def solution(mesh):
    in_specs = (
        P(None, "seg", "gx", "gy"),
        P("seg", "gx", "gy"),
        P("gx", "gy"),
        P("gx", "gy"),
        P("seg", None),
        P("seg", None),
    )
    out_specs = (P(None, "seg", "gx", "gy"), P("seg", "gx", "gy"))
    return jax.shard_map(body, mesh=mesh, in_specs=in_specs, out_specs=out_specs, check_vma=False)
```

profile of v0, /device:TPU:0, one launch (start us, length us, event | category | flops | bytes accessed | tf_op | source)
XLA Modules:
  0.0 203.1 jit_solution(5789935153862587755)
XLA Ops:
  0.6 0.9 fusion.64
  1.5 1.3 collective-permute-start
  2.8 6.1 %collective-permute-start.1 = (f32[7,1,16,128]{3,2,1,0:T(8,128)S(1)}, f32[7,1,16,128]{3,2,1,0:T(8,128)}, u32[]{:S(2)}, u32[]{:S(2)}) collective-permute-start(f32[7,1,16,128]{3,2,1,0:T(8,128)S(1)} %get-tuple-element.18), channel_id=1, source_target_pairs={{0,8},{8,16},{16,24},{1,9},{9,17},{17,25},{2,10},{10,18},{18,26},{... | collective-permute-start | bytes 172040 | tf_op jit(solution)/shard_map/ppermute | solution.py:24
  8.9 1.5 copy.47
  10.4 0.7 fusion.66
  11.1 1.3 collective-permute-start.12
  12.3 3.0 %collective-permute-start.13 = (f32[96,1,128]{0,2,1:T(8,128)S(1)}, f32[96,1,128]{0,2,1:T(8,128)S(1)}, u32[]{:S(2)}, u32[]{:S(2)}) collective-permute-start(f32[96,1,128]{0,2,1:T(8,128)S(1)} %get-tuple-element.28), channel_id=1, source_target_pairs={{0,4},{1,5},{2,6},{3,7},{8,12},{9,13},{10,14},{11,15},{16,20},{17,... | collective-permute-start | bytes 147464 | tf_op jit(solution)/shard_map/ppermute | solution.py:24
  15.6 0.7 select_add_fusion
  16.3 1.4 fusion.68
  17.8 1.4 fusion.69
  19.1 1.3 dynamic-slice
  21.0 4.0 %stack.12 = f32[6]{0:T(128)S(1)} concatenate(f32[1]{0:T(128)} %bitcast.7, f32[1]{0:T(128)} %bitcast.8, f32[1]{0:T(128)} %bitcast.9, f32[1]{0:T(128)} %bitcast.10, f32[1]{0:T(128)} %bitcast.11, f32[1]{0:T(128)} %bitcast.12), dimensions={0} | concatenate | bytes 48 | tf_op jit(solution)/shard_map/stack | solution.py:126
  25.2 7.9 %copy.27 = f32[7,96,16,128]{1,3,2,0:T(8,128)} copy(f32[7,96,16,128]{3,2,1,0:T(8,128)} %param.8) | data formatting | bytes 11010048 | tf_op args[0]
  33.1 9.7 %all-reduce = f32[24]{0:T(128)S(1)} all-reduce(f32[24]{0:T(128)S(1)} %dynamic-update-slice), channel_id=2, replica_groups=mesh['seg'=4,'gx'=2,'gy'=4] {'seg'}, use_global_device_ids=true, to_apply=%add | all-reduce | flops 24 | bytes 192
  44.3 0.6 divide_bitcast_fusion.14
  45.2 0.6 slice.381
  45.8 0.7 divide_bitcast_fusion.12
  46.5 0.7 divide_bitcast_fusion.15
  47.3 0.7 divide_bitcast_fusion.13
  48.8 0.6 divide_bitcast_fusion.10
  49.7 0.7 divide_bitcast_fusion.11
  51.0 0.6 divide_bitcast_fusion.8
  51.7 0.7 divide_bitcast_fusion.9
  53.3 0.6 divide_bitcast_fusion.6
  53.9 0.7 divide_bitcast_fusion.7
  55.5 0.6 divide_bitcast_fusion.4
  56.2 0.7 divide_bitcast_fusion.5
  57.8 0.6 divide_bitcast_fusion.2
  58.4 0.7 divide_bitcast_fusion.3
  60.0 0.6 divide_bitcast_fusion
  60.6 0.7 divide_bitcast_fusion.1
  61.6 4.5 %copy.29 = f32[7,1,16,128]{1,3,2,0:T(8,128)} copy(f32[7,1,16,128]{3,2,1,0:T(8,128)S(1)} %collective-permute-done) | data formatting | bytes 114688 | tf_op jit(solution)/shard_map/ppermute | solution.py:27
  66.1 5.2 %copy.30 = f32[7,1,16,128]{1,3,2,0:T(8,128)} copy(f32[7,1,16,128]{3,2,1,0:T(8,128)} %collective-permute-done.1) | data formatting | bytes 114688 | tf_op jit(solution)/shard_map/ppermute | solution.py:24
  71.2 2.4 %pad_maximum_fusion.33 = (f32[7,98,1,128]{1,3,2,0:T(8,128)S(1)}, f32[7,98,1,128]{1,3,2,0:T(8,128)S(1)}) fusion(f32[7,1,16,128]{1,3,2,0:T(8,128)} %copy.29, f32[7,96,16,128]{1,3,2,0:T(8,128)} %copy.27, f32[7,1,16,128]{1,3,2,0:T(8,128)} %copy.30), kind=kLoop, calls=%fused_computation.92 | loop fusion | flops 351232 | bytes 6322176 | tf_op jit(solution)/shard_map/concatenate | solution.py:28
  73.7 1.6 collective-permute-start.2
  75.2 3.1 %collective-permute-start.3 = (f32[7,98,1,128]{1,3,2,0:T(8,128)S(1)}, f32[7,98,1,128]{1,3,2,0:T(8,128)S(1)}, u32[]{:S(2)}, u32[]{:S(2)}) collective-permute-start(f32[7,98,1,128]{1,3,2,0:T(8,128)S(1)} %get-tuple-element.16), channel_id=1, source_target_pairs={{0,4},{1,5},{2,6},{3,7},{8,12},{9,13},{10,14},{11,15},{16,20},{17,... | collective-permute-start | bytes 1053704 | tf_op jit(solution)/shard_map/ppermute | solution.py:24
  78.4 1.1 fusion.40
  79.7 1.9 pad_maximum_fusion.39
  81.6 1.3 collective-permute-start.4
  82.9 4.7 %collective-permute-start.5 = (f32[7,98,18,1]{1,3,2,0:T(1,128)S(1)}, f32[7,98,18,1]{1,3,2,0:T(1,128)S(1)}, u32[]{:S(2)}, u32[]{:S(2)}) collective-permute-start(f32[7,98,18,1]{1,3,2,0:T(1,128)S(1)} %get-tuple-element.14), channel_id=1, source_target_pairs={{0,1},{1,2},{2,3},{4,5},{5,6},{6,7},{8,9},{9,10},{10,11},{12,13},{... | collective-permute-start | bytes 148184 | tf_op jit(solution)/shard_map/ppermute | solution.py:24
  87.7 0.8 fusion.44
  88.4 0.9 collective-permute-done.5
  89.4 48.4 %fusion.62 = (f32[96,16,128]{0,2,1:T(8,128)S(1)}, f32[6,96,16,128]{1,3,2,0:T(8,128)}) fusion(f32[96,16,128]{0,2,1:T(8,128)} %fusion.40, f32[6]{0:T(128)S(1)} %copy-done.13, f32[7,98,1,128]{1,3,2,0:T(8,128)} %copy-done.3, f32[7,1,16,128]{1,3,2,0:T(8,128)} %copy.29, f32[7,96,16,128]{1,3,2,0:T(8,128)} %copy.27, f32[7,1,16,128]{1,3,2,0:T(8,128)} %copy.30, ...), kind=kLoop, calls=%fused_computation.222 | loop fusion | flops 38731776 | bytes 35881488 | tf_op jit(solution)/shard_map/reduce_sum | solution.py:118
  138.6 1.7 collective-permute-start.6
  140.6 1.3 collective-permute-start.7
  141.9 0.7 slice_reduce_fusion.1
  143.0 4.3 %collective-permute-done.7 = f32[1,16,128]{2,1,0:T(8,128)S(1)} collective-permute-done((f32[1,16,128]{2,1,0:T(8,128)S(1)}, f32[1,16,128]{2,1,0:T(8,128)S(1)}, u32[]{:S(2)}, u32[]{:S(2)}) %collective-permute-start.7) | collective-permute-done | bytes 8224 | tf_op jit(solution)/shard_map/ppermute | solution.py:27
  147.9 1.4 collective-permute-start.8
  149.3 1.3 collective-permute-start.9
  150.6 0.9 pad_maximum_fusion.46
  151.5 1.3 collective-permute-start.14
  152.8 4.9 %collective-permute-start.15 = (f32[96,18,1]{0,2,1:T(1,128)S(1)}, f32[96,18,1]{0,2,1:T(1,128)S(1)}, u32[]{:S(2)}, u32[]{:S(2)}) collective-permute-start(f32[96,18,1]{0,2,1:T(1,128)S(1)} %get-tuple-element.25), channel_id=1, source_target_pairs={{0,1},{1,2},{2,3},{4,5},{5,6},{6,7},{8,9},{9,10},{10,11},{12,13},{... | collective-permute-start | bytes 20744 | tf_op jit(solution)/shard_map/ppermute | solution.py:24
  157.9 3.9 %collective-permute-start.10 = (f32[98,18,1]{0,2,1:T(1,128)S(1)}, f32[98,18,1]{0,2,1:T(1,128)S(1)}, u32[]{:S(2)}, u32[]{:S(2)}) collective-permute-start(f32[98,18,1]{0,2,1:T(1,128)S(1)} %get-tuple-element.20), channel_id=1, source_target_pairs={{0,1},{1,2},{2,3},{4,5},{5,6},{6,7},{8,9},{9,10},{10,11},{12,13},{... | collective-permute-start | bytes 21176 | tf_op jit(solution)/shard_map/ppermute | solution.py:24
  161.8 1.6 collective-permute-start.11
  163.5 2.5 %fusion.10 = f32[98,18,130]{0,2,1:T(8,128)S(1)} fusion(f32[7,98,18,1]{1,3,2,0:T(1,128)S(1)} %collective-permute-done.4, f32[7,98,18,1]{1,3,2,0:T(1,128)S(1)} %collective-permute-done.5, f32[7,98,1,128]{1,3,2,0:T(8,128)S(1)} %copy-done.4, f32[7,98,1,128]{1,3,2,0:T(8,128)S(1)} %copy-done.6, f32[7,1,16,128]{1,3,2,0:T(8,128)} %copy.29, ...), kind=kLoop, calls=%fused_computation.32 | loop fusion | flops 1375920 | bytes 7338240 | tf_op jit(solution)/shard_map/squeeze | solution.py:120
  166.0 1.5 collective-permute-done.11
  167.5 0.7 fusion.11
  168.2 6.2 %fusion.16 = (f32[96,16,128]{0,2,1:T(8,128)S(1)}, f32[96,16,128]{0,2,1:T(8,128)S(1)}) fusion(f32[96,16,128]{0,2,1:T(8,128)S(1)} %copy-done.2, f32[96,18,1]{0,2,1:T(1,128)S(1)} %collective-permute-done.15, f32[96,1,128]{0,2,1:T(8,128)S(1)} %collective-permute-done.12, f32[96,1,128]{0,2,1:T(8,128)S(1)} %collective-permute-done.13, ...), kind=kLoop, calls=%fused_computation.45 | loop fusion | flops 10813440 | bytes 15078912 | tf_op jit(solution)/shard_map/add | solution.py:80
  174.5 1.2 convolution_bitcast_fusion
  175.7 9.6 %all-gather.1 = f32[4,2,2048]{2,1,0:T(2,128)S(1)} all-gather(f32[1,2,2048]{2,1,0:T(2,128)S(1)} %maximum_bitcast_fusion), channel_id=1, replica_groups=mesh['seg'=4,'gx'=2,'gy'=4] {'seg'}, dimensions={0}, use_global_device_ids=true | all-gather | bytes 81920 | tf_op jit(solution)/shard_map/all_gather | solution.py:138
  185.6 1.3 slice_multiply_fusion.3
  187.1 1.0 copy.50
  188.1 7.0 %pad_maximum_fusion = f32[7,96,16,128]{1,3,2,0:T(8,128)} fusion(f32[1,96,16,128]{1,3,2,0:T(8,128)S(1)} %bitcast.73, f32[6,96,16,128]{1,3,2,0:T(8,128)} %get-tuple-element.13), kind=kLoop, calls=%fused_computation.1 | loop fusion | flops 1376256 | bytes 11010048 | tf_op jit(solution)/shard_map/concatenate | solution.py:122
  195.2 7.9 %copy.49 = f32[7,96,16,128]{3,2,1,0:T(8,128)} copy(f32[7,96,16,128]{1,3,2,0:T(8,128)} %pad_maximum_fusion) | data formatting | bytes 11010048
  (107 shorter events, 10.7 us)
Async XLA Ops:
  1.5 60.1 %collective-permute-start = (f32[7,1,16,128]{3,2,1,0:T(8,128)S(1)}, f32[7,1,16,128]{3,2,1,0:T(8,128)S(1)}, u32[]{:S(2)}, u32[]{:S(2)}) collective-permute-start(f32[7,1,16,128]{3,2,1,0:T(8,128)S(1)} %get-tuple-element.19), channel_id=1, source_target_pairs={{8,0},{16,8},{24,16},{9,1},{17,9},{25,17},{10,2},{18,10},{26,18},{... | collective-permute-start | bytes 172040 | tf_op jit(solution)/shard_map/ppermute | solution.py:27
  2.8 63.3 %collective-permute-start.1 = (f32[7,1,16,128]{3,2,1,0:T(8,128)S(1)}, f32[7,1,16,128]{3,2,1,0:T(8,128)}, u32[]{:S(2)}, u32[]{:S(2)}) collective-permute-start(f32[7,1,16,128]{3,2,1,0:T(8,128)S(1)} %get-tuple-element.18), channel_id=1, source_target_pairs={{0,8},{8,16},{16,24},{1,9},{9,17},{17,25},{2,10},{10,18},{18,26},{... | collective-permute-start | bytes 172040 | tf_op jit(solution)/shard_map/ppermute | solution.py:24
  10.4 22.7 %copy-start.1 = (f32[96,16,128]{0,2,1:T(8,128)}, f32[96,16,128]{0,2,1:T(8,128)S(1)}, u32[]{:S(2)}) copy-start(f32[96,16,128]{0,2,1:T(8,128)S(1)} %copy.47) | copy-start | bytes 2359300
  11.1 139.5 %collective-permute-start.12 = (f32[96,1,128]{0,2,1:T(8,128)}, f32[96,1,128]{0,2,1:T(8,128)S(1)}, u32[]{:S(2)}, u32[]{:S(2)}) collective-permute-start(f32[96,1,128]{0,2,1:T(8,128)} %get-tuple-element.29), channel_id=1, source_target_pairs={{4,0},{5,1},{6,2},{7,3},{12,8},{13,9},{14,10},{15,11},{20,16},{21,... | collective-permute-start | bytes 147464 | tf_op jit(solution)/shard_map/ppermute | solution.py:27
  12.3 138.3 %collective-permute-start.13 = (f32[96,1,128]{0,2,1:T(8,128)S(1)}, f32[96,1,128]{0,2,1:T(8,128)S(1)}, u32[]{:S(2)}, u32[]{:S(2)}) collective-permute-start(f32[96,1,128]{0,2,1:T(8,128)S(1)} %get-tuple-element.28), channel_id=1, source_target_pairs={{0,4},{1,5},{2,6},{3,7},{8,12},{9,13},{10,14},{11,15},{16,20},{17,... | collective-permute-start | bytes 147464 | tf_op jit(solution)/shard_map/ppermute | solution.py:24
  66.1 12.3 %slice-start = ((s8[7340032]{0:T(1024)(128)(4,1)}), s8[3145728]{0:T(1024)(128)(4,1)S(1)}, s32[]{:S(2)}) async-start(s8[7340032]{0:T(1024)(128)(4,1)} %bitcast.71), calls=%async_computation | async-start | bytes 6291456
  71.2 7.1 %slice-start.1 = ((s8[7340032]{0:T(1024)(128)(4,1)}), s8[4194304]{0:T(1024)(128)(4,1)S(1)}, s32[]{:S(2)}) async-start(s8[7340032]{0:T(1024)(128)(4,1)} %bitcast.71), calls=%async_computation.1 | async-start | bytes 8388608
  71.2 8.5 %copy-start = (f32[7,1,16,128]{1,3,2,0:T(8,128)S(1)}, f32[7,1,16,128]{1,3,2,0:T(8,128)}, u32[]{:S(2)}) copy-start(f32[7,1,16,128]{1,3,2,0:T(8,128)} %copy.30) | copy-start | bytes 172036
  73.7 5.8 %collective-permute-start.2 = (f32[7,98,1,128]{1,3,2,0:T(8,128)S(1)}, f32[7,98,1,128]{1,3,2,0:T(8,128)S(1)}, u32[]{:S(2)}, u32[]{:S(2)}) collective-permute-start(f32[7,98,1,128]{1,3,2,0:T(8,128)S(1)} %get-tuple-element.17), channel_id=1, source_target_pairs={{4,0},{5,1},{6,2},{7,3},{12,8},{13,9},{14,10},{15,11},{20,16},{21,... | collective-permute-start | bytes 1053704 | tf_op jit(solution)/shard_map/ppermute | solution.py:27
  75.2 4.5 %collective-permute-start.3 = (f32[7,98,1,128]{1,3,2,0:T(8,128)S(1)}, f32[7,98,1,128]{1,3,2,0:T(8,128)S(1)}, u32[]{:S(2)}, u32[]{:S(2)}) collective-permute-start(f32[7,98,1,128]{1,3,2,0:T(8,128)S(1)} %get-tuple-element.16), channel_id=1, source_target_pairs={{0,4},{1,5},{2,6},{3,7},{8,12},{9,13},{10,14},{11,15},{16,20},{17,... | collective-permute-start | bytes 1053704 | tf_op jit(solution)/shard_map/ppermute | solution.py:24
  79.5 9.9 %copy-start.12 = (f32[6]{0:T(128)S(1)}, f32[6]{0:T(128)}, u32[]{:S(2)}) copy-start(f32[6]{0:T(128)} %constant.83.clone) | copy-start | bytes 76
  79.5 9.9 %copy-start.13 = (f32[6]{0:T(128)S(1)}, f32[6]{0:T(128)}, u32[]{:S(2)}) copy-start(f32[6]{0:T(128)} %constant.84.clone) | copy-start | bytes 76
  79.5 2.1 %copy-start.3 = (f32[7,98,1,128]{1,3,2,0:T(8,128)}, f32[7,98,1,128]{1,3,2,0:T(8,128)S(1)}, u32[]{:S(2)}) copy-start(f32[7,98,1,128]{1,3,2,0:T(8,128)S(1)} %collective-permute-done.2) | copy-start | bytes 1053700
  79.7 1.9 copy-start.5
  81.6 6.8 %collective-permute-start.4 = (f32[7,98,18,1]{1,3,2,0:T(1,128)S(1)}, f32[7,98,18,1]{1,3,2,0:T(1,128)S(1)}, u32[]{:S(2)}, u32[]{:S(2)}) collective-permute-start(f32[7,98,18,1]{1,3,2,0:T(1,128)S(1)} %get-tuple-element.15), channel_id=1, source_target_pairs={{1,0},{2,1},{3,2},{5,4},{6,5},{7,6},{9,8},{10,9},{11,10},{13,12},{... | collective-permute-start | bytes 148184 | tf_op jit(solution)/shard_map/ppermute | solution.py:27
  82.9 6.4 %collective-permute-start.5 = (f32[7,98,18,1]{1,3,2,0:T(1,128)S(1)}, f32[7,98,18,1]{1,3,2,0:T(1,128)S(1)}, u32[]{:S(2)}, u32[]{:S(2)}) collective-permute-start(f32[7,98,18,1]{1,3,2,0:T(1,128)S(1)} %get-tuple-element.14), channel_id=1, source_target_pairs={{0,1},{1,2},{2,3},{4,5},{5,6},{6,7},{8,9},{9,10},{10,11},{12,13},{... | collective-permute-start | bytes 148184 | tf_op jit(solution)/shard_map/ppermute | solution.py:24
  137.8 4.1 %copy-start.7 = (f32[96,96]{1,0:T(8,128)S(1)}, f32[96,96]{1,0:T(8,128)}, u32[]{:S(2)}) copy-start(f32[96,96]{1,0:T(8,128)} %param.12) | copy-start | bytes 110596
  138.6 4.0 %collective-permute-start.6 = (f32[1,16,128]{2,1,0:T(8,128)S(1)}, f32[1,16,128]{2,1,0:T(8,128)S(1)}, u32[]{:S(2)}, u32[]{:S(2)}) collective-permute-start(f32[1,16,128]{2,1,0:T(8,128)S(1)} %copy.37), channel_id=1, source_target_pairs={{0,8},{8,16},{16,24},{1,9},{9,17},{17,25},{2,10},{10,18},{18,26},{... | collective-permute-start | bytes 24584 | tf_op jit(solution)/shard_map/ppermute | solution.py:24
  140.6 6.7 %collective-permute-start.7 = (f32[1,16,128]{2,1,0:T(8,128)S(1)}, f32[1,16,128]{2,1,0:T(8,128)S(1)}, u32[]{:S(2)}, u32[]{:S(2)}) collective-permute-start(f32[1,16,128]{2,1,0:T(8,128)S(1)} %copy.38), channel_id=1, source_target_pairs={{8,0},{16,8},{24,16},{9,1},{17,9},{25,17},{10,2},{18,10},{26,18},{... | collective-permute-start | bytes 24584 | tf_op jit(solution)/shard_map/ppermute | solution.py:27
  147.7 15.8 %copy-start.4 = (f32[7,98,1,128]{1,3,2,0:T(8,128)S(1)}, f32[7,98,1,128]{1,3,2,0:T(8,128)}, u32[]{:S(2)}) copy-start(f32[7,98,1,128]{1,3,2,0:T(8,128)} %copy-done.3) | copy-start | bytes 1053700
  147.7 15.8 %copy-start.6 = (f32[7,98,1,128]{1,3,2,0:T(8,128)S(1)}, f32[7,98,1,128]{1,3,2,0:T(8,128)}, u32[]{:S(2)}) copy-start(f32[7,98,1,128]{1,3,2,0:T(8,128)} %copy-done.5) | copy-start | bytes 1053700
  147.9 9.9 %collective-permute-start.8 = (f32[98,1,128]{0,2,1:T(8,128)S(1)}, f32[98,1,128]{0,2,1:T(8,128)S(1)}, u32[]{:S(2)}, u32[]{:S(2)}) collective-permute-start(f32[98,1,128]{0,2,1:T(8,128)S(1)} %get-tuple-element.22), channel_id=1, source_target_pairs={{0,4},{1,5},{2,6},{3,7},{8,12},{9,13},{10,14},{11,15},{16,20},{17,... | collective-permute-start | bytes 150536 | tf_op jit(solution)/shard_map/ppermute | solution.py:24
  149.3 8.4 %collective-permute-start.9 = (f32[98,1,128]{0,2,1:T(8,128)S(1)}, f32[98,1,128]{0,2,1:T(8,128)S(1)}, u32[]{:S(2)}, u32[]{:S(2)}) collective-permute-start(f32[98,1,128]{0,2,1:T(8,128)S(1)} %get-tuple-element.23), channel_id=1, source_target_pairs={{4,0},{5,1},{6,2},{7,3},{12,8},{13,9},{14,10},{15,11},{20,16},{21,... | collective-permute-start | bytes 150536 | tf_op jit(solution)/shard_map/ppermute | solution.py:27
  151.5 16.7 %collective-permute-start.14 = (f32[96,18,1]{0,2,1:T(1,128)S(1)}, f32[96,18,1]{0,2,1:T(1,128)S(1)}, u32[]{:S(2)}, u32[]{:S(2)}) collective-permute-start(f32[96,18,1]{0,2,1:T(1,128)S(1)} %get-tuple-element.24), channel_id=1, source_target_pairs={{1,0},{2,1},{3,2},{5,4},{6,5},{7,6},{9,8},{10,9},{11,10},{13,12},{... | collective-permute-start | bytes 20744 | tf_op jit(solution)/shard_map/ppermute | solution.py:27
  152.8 15.4 %collective-permute-start.15 = (f32[96,18,1]{0,2,1:T(1,128)S(1)}, f32[96,18,1]{0,2,1:T(1,128)S(1)}, u32[]{:S(2)}, u32[]{:S(2)}) collective-permute-start(f32[96,18,1]{0,2,1:T(1,128)S(1)} %get-tuple-element.25), channel_id=1, source_target_pairs={{0,1},{1,2},{2,3},{4,5},{5,6},{6,7},{8,9},{9,10},{10,11},{12,13},{... | collective-permute-start | bytes 20744 | tf_op jit(solution)/shard_map/ppermute | solution.py:24
  157.9 8.1 %collective-permute-start.10 = (f32[98,18,1]{0,2,1:T(1,128)S(1)}, f32[98,18,1]{0,2,1:T(1,128)S(1)}, u32[]{:S(2)}, u32[]{:S(2)}) collective-permute-start(f32[98,18,1]{0,2,1:T(1,128)S(1)} %get-tuple-element.20), channel_id=1, source_target_pairs={{0,1},{1,2},{2,3},{4,5},{5,6},{6,7},{8,9},{9,10},{10,11},{12,13},{... | collective-permute-start | bytes 21176 | tf_op jit(solution)/shard_map/ppermute | solution.py:24
  161.8 6.4 %copy-start.2 = (f32[96,16,128]{0,2,1:T(8,128)S(1)}, f32[96,16,128]{0,2,1:T(8,128)}, u32[]{:S(2)}) copy-start(f32[96,16,128]{0,2,1:T(8,128)} %copy-done.1) | copy-start | bytes 2359300
  161.8 6.4 %copy-start.8 = (f32[16,128]{1,0:T(8,128)S(1)}, f32[16,128]{1,0:T(8,128)}, u32[]{:S(2)}) copy-start(f32[16,128]{1,0:T(8,128)} %param.10) | copy-start | bytes 24580
  161.8 5.7 %collective-permute-start.11 = (f32[98,18,1]{0,2,1:T(1,128)S(1)}, f32[98,18,1]{0,2,1:T(1,128)S(1)}, u32[]{:S(2)}, u32[]{:S(2)}) collective-permute-start(f32[98,18,1]{0,2,1:T(1,128)S(1)} %get-tuple-element.21), channel_id=1, source_target_pairs={{1,0},{2,1},{3,2},{5,4},{6,5},{7,6},{9,8},{10,9},{11,10},{13,12},{... | collective-permute-start | bytes 21176 | tf_op jit(solution)/shard_map/ppermute | solution.py:27
  168.2 17.2 %copy-start.11 = (f32[2,8]{1,0:T(2,128)S(1)}, f32[2,8]{1,0:T(2,128)}, u32[]{:S(2)}) copy-start(f32[2,8]{1,0:T(2,128)} %fusion.44) | copy-start | bytes 196
  168.2 18.7 %copy-start.9 = (f32[96]{0:T(128)S(1)}, f32[96]{0:T(128)}, u32[]{:S(2)}) copy-start(f32[96]{0:T(128)} %get-tuple-element.6) | copy-start | bytes 1156
  168.2 18.7 %copy-start.10 = (f32[96]{0:T(128)S(1)}, f32[96]{0:T(128)}, u32[]{:S(2)}) copy-start(f32[96]{0:T(128)} %get-tuple-element.7) | copy-start | bytes 1156
where the time goes:
time: 204 us; the launch traced here: 203 us
  other arithmetic  87.1 us (43%)
  local copies, waits for them, and re-layouts  45.7 us (22%)
  starting transfers between devices  39.8 us (20%)
  blocking collectives  19.4 us (10%)
  waiting for transfers between devices  6.94 us (3%)
  matrix products  2.19 us (1%)
    reduce_sum x1, other arithmetic, body(): mix = 0.5 * jnp.sum(species_new, axis=0)  48.4 us
    ppermute x8, starting transfers between devices, with_halo(): lax.ppermute(lax.slice_in_dim(block, block.shape[dim] - width, None, axis...  28.9 us
    unnamed x40, local copies, waits for them, and re-layouts  19.9 us
    ppermute x8, starting transfers between devices, with_halo(): lax.ppermute(lax.slice_in_dim(block, 0, width, axis=dim), axis, backward)  10.9 us
    unnamed x1, blocking collectives  9.74 us
    all_gather x1, blocking collectives, body(): lax.all_gather(ends, 'seg', axis=0, tiled=True)  9.64 us
    concatenate x1, other arithmetic, body(): gas_next = jnp.concatenate([species_new, heat_new[None]], axis=0)  7.02 us
    add x1, other arithmetic, solid_source(): temp + lateral * (beside - 4.0 * temp) + exchange[None] * (heat_new - temp)  6.22 us
  transfers between devices with their start and end apart: 16, of which 4 were waited for; matrix products, arithmetic and copies ran while one was open for 54% of the time, Pallas kernels for 0%

commit v1 on v0

v1 whole, which is shorter than its diff:
```python
import jax
import jax.numpy as jnp
from jax import lax
from jax.experimental import pallas as pl
from jax.experimental.pallas import tpu as pltpu
from jax.sharding import PartitionSpec as P

diffusion = (0.1, 0.08, 0.12, 0.09, 0.11, 0.07)
stoich = (-1.0, -0.5, 1.0, 0.5, 0.25, 0.75)
rate_const = 0.3
upwind = 0.25
cond_base = 0.04
cond_slope = 0.3
heat_release = 0.5
lateral = 0.1
loss_table = (0.0, 0.3, 0.0, 0.1)
feed_table = (0.0, 0.0, 0.4, 0.0)
highest = lax.Precision.HIGHEST


MESH = pl.DeviceIdType.MESH
VMEM = pl.BlockSpec(memory_space=pltpu.VMEM)
ANY = pl.BlockSpec(memory_space=pl.ANY)
F32 = jnp.float32
CHUNK = 16


def shape(*dims):
    return jax.ShapeDtypeStruct(dims, F32)


def params():
    return pltpu.CompilerParams(vmem_limit_bytes=48 * 1024 * 1024)


def iotas(rows, lanes):
    row = lax.broadcasted_iota(jnp.int32, (rows, lanes), 0)
    lane = lax.broadcasted_iota(jnp.int32, (rows, lanes), 1)
    return row, lane


def pack_columns(packed, plane, z, lane, last):
    lanes = plane.shape[1]
    moved = pltpu.roll(plane, lax.rem(z + 1, lanes) if last else z, 1)
    return jnp.where(lane == z, moved, packed)


def shifted(plane, row, lane, z, xlo, xhi, ylo, yhi):
    rows, lanes = plane.shape
    west = jnp.where(row == 0, xlo, pltpu.roll(plane, 1, 0))
    east = jnp.where(row == rows - 1, xhi, pltpu.roll(plane, rows - 1, 0))
    low_col = pltpu.roll(ylo, lax.rem(lanes - z, lanes), 1)
    high_col = pltpu.roll(yhi, lanes - 1 - z, 1)
    south = jnp.where(lane == 0, low_col, pltpu.roll(plane, 1, 1))
    north = jnp.where(lane == lanes - 1, high_col, pltpu.roll(plane, lanes - 1, 1))
    return west, east, south, north


def pack_kernel(gas, temp, x_first, x_last, y_first, y_last):
    step = pl.program_id(0)
    fields = gas.shape[0] + 1
    rows, lanes = gas.shape[2:]
    _, lane = iotas(rows, lanes)

    @pl.when(step == 0)
    def _():
        y_first[...] = jnp.zeros_like(y_first)
        y_last[...] = jnp.zeros_like(y_last)

    for field in range(fields):
        first, last = y_first[field], y_last[field]
        for k in range(gas.shape[1]):
            z = step * gas.shape[1] + k
            plane = gas[field, k] if field < fields - 1 else temp[k]
            first = pack_columns(first, plane, z, lane, False)
            last = pack_columns(last, plane, z, lane, True)
            x_first[field, k : k + 1] = plane[0:1]
            x_last[field, k : k + 1] = plane[rows - 1 : rows]
        y_first[field] = first
        y_last[field] = last


def swap_faces(axes, send_sem, recv_sem):
    barrier = pltpu.get_barrier_semaphore()
    places = []
    for name, *_ in axes:
        here, count = lax.axis_index(name), lax.axis_size(name)
        places.append((here, here > 0, here < count - 1))
    for (name, *_), (here, down, up) in zip(axes, places):
        for exists, step in ((down, -1), (up, 1)):

            @pl.when(exists)
            def _(name=name, here=here, step=step):
                pl.semaphore_signal(barrier, inc=1, device_id={name: here + step}, device_id_type=MESH)

    peers = sum(exists.astype(jnp.int32) for _, *both in places for exists in both)
    pl.semaphore_wait(barrier, peers)

    plan = []
    for index, ((name, first, last, low, high), (here, down, up)) in enumerate(zip(axes, places)):
        to_up = pltpu.make_async_remote_copy(
            src_ref=last, dst_ref=low, send_sem=send_sem.at[2 * index], recv_sem=recv_sem.at[2 * index],
            device_id={name: here + 1}, device_id_type=MESH)
        to_down = pltpu.make_async_remote_copy(
            src_ref=first, dst_ref=high, send_sem=send_sem.at[2 * index + 1], recv_sem=recv_sem.at[2 * index + 1],
            device_id={name: here - 1}, device_id_type=MESH)
        plan.append((to_up, to_down, down, up, low, high))
    for to_up, to_down, down, up, low, high in plan:
        pl.when(up)(to_up.start)
        pl.when(down)(to_down.start)
    for to_up, to_down, down, up, low, high in plan:

        @pl.when(jnp.logical_not(down))
        def _(low=low):
            low[...] = jnp.zeros(low.shape, F32)

        @pl.when(jnp.logical_not(up))
        def _(high=high):
            high[...] = jnp.zeros(high.shape, F32)

    for to_up, to_down, down, up, low, high in plan:
        pl.when(up)(to_up.wait_send)
        pl.when(down)(to_down.wait_send)
        pl.when(down)(to_up.wait_recv)
        pl.when(up)(to_down.wait_recv)


def swap_gas_kernel(z_first, z_last, x_first, x_last, y_first, y_last, zlo, zhi, xlo, xhi, ylo, yhi, send_sem, recv_sem):
    swap_faces(
        (
            ("gx", x_first, x_last, xlo, xhi),
            ("seg", z_first, z_last, zlo, zhi),
            ("gy", y_first, y_last, ylo, yhi),
        ),
        send_sem,
        recv_sem,
    )


def swap(z_first, z_last, x_first, x_last, y_first, y_last, ident):
    faces = (z_first, z_last, x_first, x_last, y_first, y_last)
    return pl.pallas_call(
        swap_gas_kernel,
        out_shape=[shape(*face.shape) for face in faces],
        in_specs=[VMEM] * 6,
        out_specs=[VMEM] * 6,
        scratch_shapes=[pltpu.SemaphoreType.DMA((6,)), pltpu.SemaphoreType.DMA((6,))],
        compiler_params=pltpu.CompilerParams(collective_id=ident, has_side_effects=True),
    )(*faces)


def species_kernel(
    gas, before, after, zlo, zhi, xlo, xhi, ylo, yhi, new, mix_out, z_first, z_last, x_first, x_last, y_first, y_last
):
    step, steps = pl.program_id(0), pl.num_programs(0)
    count, depth, rows, lanes = gas.shape
    row, lane = iotas(rows, lanes)
    at_bottom, at_top = step == 0, step == steps - 1

    @pl.when(step == 0)
    def _():
        y_first[...] = jnp.zeros_like(y_first)
        y_last[...] = jnp.zeros_like(y_last)

    first, last = y_first[...], y_last[...]
    for k in range(depth):
        z = step * depth + k
        reaction = rate_const * gas[0, k] * gas[1, k]
        total = None
        for s in range(count):
            center = gas[s, k]
            below = gas[s, k - 1] if k > 0 else jnp.where(at_bottom, zlo[s], before[s, 0])
            above = gas[s, k + 1] if k < depth - 1 else jnp.where(at_top, zhi[s], after[s, 0])
            west, east, south, north = shifted(
                center, row, lane, z, xlo[s, k : k + 1], xhi[s, k : k + 1], ylo[s], yhi[s]
            )
            beside = (below + above) + (west + east) + (south + north)
            value = (
                center
                + diffusion[s] * (beside - 6.0 * center)
                - upwind * (center - below)
                + stoich[s] * reaction
            )
            new[s, k] = value
            total = value if total is None else total + value
        mix = 0.5 * total
        mix_out[k] = mix
        first = pack_columns(first, mix, z, lane, False)
        last = pack_columns(last, mix, z, lane, True)
        x_first[k : k + 1] = mix[0:1]
        x_last[k : k + 1] = mix[rows - 1 : rows]
        if k == 0:

            @pl.when(at_bottom)
            def _(mix=mix):
                z_first[...] = mix

        if k == depth - 1:

            @pl.when(at_top)
            def _(mix=mix):
                z_last[...] = mix

    y_first[...] = first
    y_last[...] = last


def lookup(flags, table):
    result = jnp.zeros(flags.shape, F32)
    for value, entry in enumerate(table):
        result = result + jnp.where(flags == value, entry, 0.0)
    return result


def energy_kernel(
    pair, heat, heat_before, heat_after, mix, mix_before, mix_after, temp, exchange, flags, inverse, coupling,
    zlo, zhi, xlo, xhi, ylo, yhi, mzlo, mzhi, mxlo, mxhi, mylo, myhi, gas_in,
    heat_out, local, ends, source,
):
    step, steps = pl.program_id(0), pl.num_programs(0)
    depth, rows, lanes = temp.shape
    row, lane = iotas(rows, lanes)
    at_bottom, at_top = step == 0, step == steps - 1
    loss = lookup(flags[...], loss_table)
    feed = lookup(flags[...], feed_table)
    rate = exchange[...]
    for k in range(depth):
        z = step * depth + k
        reaction = rate_const * pair[0, k] * pair[1, k]
        heat_mid, mix_mid, temp_mid = heat[0, k], mix[k], temp[k]
        heat_below = heat[0, k - 1] if k > 0 else jnp.where(at_bottom, zlo[6], heat_before[0, 0])
        heat_above = heat[0, k + 1] if k < depth - 1 else jnp.where(at_top, zhi[6], heat_after[0, 0])
        mix_below = mix[k - 1] if k > 0 else jnp.where(at_bottom, mzlo[...], mix_before[0])
        mix_above = mix[k + 1] if k < depth - 1 else jnp.where(at_top, mzhi[...], mix_after[0])
        one = slice(k, k + 1)
        heats = (heat_below, heat_above) + shifted(
            heat_mid, row, lane, z, xlo[6, one], xhi[6, one], ylo[6], yhi[6]
        )
        mixes = (mix_below, mix_above) + shifted(
            mix_mid, row, lane, z, mxlo[one], mxhi[one], mylo[...], myhi[...]
        )
        temps = shifted(temp_mid, row, lane, z, xlo[7, one], xhi[7, one], ylo[7], yhi[7])
        cond_mid = cond_base + cond_slope * mix_mid
        flux = None
        for heat_near, mix_near in zip(heats, mixes):
            part = (cond_mid + (cond_base + cond_slope * mix_near)) * (heat_near - heat_mid)
            flux = part if flux is None else flux + part
        heat_new = heat_mid + 0.5 * flux + heat_release * reaction - loss * heat_mid + feed
        heat_out[0, k] = heat_new
        beside = (temps[0] + temps[1]) + (temps[2] + temps[3])
        planes = temp_mid + lateral * (beside - 4.0 * temp_mid) + rate * (heat_new - temp_mid)
        source[pl.ds(pl.multiple_of(z * rows, rows), rows), :] = planes

    @pl.when(at_top)
    def _():
        size = inverse.shape[0]
        group = 4
        for start in range(0, rows, group):
            right = jnp.concatenate(
                [source[pl.ds(start + j, size, stride=rows), :] for j in range(group)], axis=1
            )
            result = jnp.dot(inverse[...], right, precision=highest, preferred_element_type=F32)
            for j in range(group):
                local[pl.ds(start + j, size, stride=rows), :] = result[:, j * lanes : (j + 1) * lanes]
        ends[0:rows] = local[0:rows]
        ends[rows : 2 * rows] = local[(size - 1) * rows : size * rows]
        scalars = (
            inverse[0:1, 0:1],
            inverse[size - 1 : size, 0:1],
            inverse[0:1, size - 1 : size],
            inverse[size - 1 : size, size - 1 : size],
            coupling[0:1, 0:1],
            coupling[0:1, 1:2],
        )
        for index, scalar in enumerate(scalars):
            ends[2 * rows + index : 2 * rows + index + 1] = jnp.broadcast_to(scalar, (1, lanes))
        ends[2 * rows + 6 : 2 * rows + 8] = jnp.zeros((2, lanes), F32)


def share_kernel(ends, slots, send_sem, recv_sem):
    here, count = lax.axis_index("seg"), lax.axis_size("seg")
    barrier = pltpu.get_barrier_semaphore()
    for step in range(1, count):
        pl.semaphore_signal(
            barrier, inc=1, device_id={"seg": lax.rem(here + step, count)}, device_id_type=MESH)
    pl.semaphore_wait(barrier, count - 1)
    copies = [
        pltpu.make_async_remote_copy(
            src_ref=ends, dst_ref=slots.at[step], send_sem=send_sem.at[step], recv_sem=recv_sem.at[step],
            device_id={"seg": lax.rem(here + step, count)}, device_id_type=MESH)
        for step in range(1, count)
    ]
    for copy in copies:
        copy.start()
    slots[0] = ends[...]
    for copy in copies:
        copy.wait()


def finish_kernel(slots, local, inverse, out):
    count, total_rows, lanes = slots.shape
    rows = (total_rows - 8) // 2
    size = inverse.shape[0]
    here = lax.axis_index("seg")
    held = [slots[lax.rem(here - s + count, count)] for s in range(count)]
    p_lines, q_lines = [], []
    for s in range(count):
        y_first, y_last = held[s][0:rows], held[s][rows : 2 * rows]
        b00, b90, b09, b99, lower, upper = (held[s][2 * rows + j : 2 * rows + j + 1] for j in range(6))
        p_gain = upper * b09 if s < count - 1 else jnp.zeros_like(upper)
        q_gain = upper * b99 if s < count - 1 else jnp.zeros_like(upper)
        p_const, q_const = y_first, y_last
        if s > 0:
            before_const, before_gain = q_lines[-1]
            into_p, into_q = lower * b00, lower * b90
            scale = 1.0 / (1.0 - into_p * before_gain)
            p_const = (y_first + into_p * before_const) * scale
            p_gain = p_gain * scale
            link = into_q * before_gain
            q_const = y_last + into_q * before_const + link * p_const
            q_gain = q_gain + link * p_gain
        p_lines.append((p_const, p_gain))
        q_lines.append((q_const, q_gain))
    firsts, lasts = [None] * count, [None] * count
    above = jnp.zeros((rows, lanes), F32)
    for s in reversed(range(count)):
        firsts[s] = p_lines[s][0] + p_lines[s][1] * above
        lasts[s] = q_lines[s][0] + q_lines[s][1] * above
        above = firsts[s]
    q_near = jnp.zeros((rows, lanes), F32)
    p_near = jnp.zeros((rows, lanes), F32)
    for s in range(count):
        if s > 0:
            q_near = jnp.where(here == s, lasts[s - 1], q_near)
        if s < count - 1:
            p_near = jnp.where(here == s, firsts[s + 1], p_near)
    mine = slots[0]
    q_near = mine[2 * rows + 4 : 2 * rows + 5] * q_near
    p_near = mine[2 * rows + 5 : 2 * rows + 6] * p_near
    for z in range(size):
        low = jnp.broadcast_to(inverse[z : z + 1, 0:1], (1, lanes))
        high = jnp.broadcast_to(inverse[z : z + 1, size - 1 : size], (1, lanes))
        block = slice(z * rows, (z + 1) * rows)
        out[block] = local[block] + q_near * low + p_near * high


def body(gas_state, solids_temp, exchange_rate, column_flags, block_inverse, line_coupling):
    count = gas_state.shape[0] - 1
    depth, rows, lanes = solids_temp.shape
    segments = lax.axis_size("seg")
    steps = depth // CHUNK
    fields = count + 2

    def fixed(*dims):
        return pl.BlockSpec(dims, lambda i: (0,) * len(dims))

    def stack(number, start):
        return pl.BlockSpec((number, CHUNK, rows, lanes), lambda i: (start, i, 0, 0))

    def below_of(number, start):
        return pl.BlockSpec(
            (number, 1, rows, lanes), lambda i: (start, jnp.maximum(i * CHUNK - 1, 0), 0, 0))

    def above_of(number, start):
        return pl.BlockSpec(
            (number, 1, rows, lanes), lambda i: (start, jnp.minimum((i + 1) * CHUNK, depth - 1), 0, 0))

    planes = pl.BlockSpec((CHUNK, rows, lanes), lambda i: (i, 0, 0))
    edge = pl.BlockSpec((CHUNK, lanes), lambda i: (i, 0))
    edges = pl.BlockSpec((fields, CHUNK, lanes), lambda i: (0, i, 0))
    sides = fixed(fields, rows, lanes)
    tops = fixed(count + 1, rows, lanes)
    side = fixed(rows, lanes)

    x_first, x_last, y_first, y_last = pl.pallas_call(
        pack_kernel,
        grid=(steps,),
        out_shape=[shape(fields, depth, lanes)] * 2 + [shape(fields, rows, lanes)] * 2,
        in_specs=[stack(count + 1, 0), planes],
        out_specs=[edges, edges, sides, sides],
        compiler_params=params(),
    )(gas_state, solids_temp)
    zlo, zhi, xlo, xhi, ylo, yhi = swap(
        gas_state[:, 0], gas_state[:, depth - 1], x_first, x_last, y_first, y_last, 0
    )
    gas_next, mix, mz_first, mz_last, mx_first, mx_last, my_first, my_last = pl.pallas_call(
        species_kernel,
        grid=(steps,),
        out_shape=[shape(count + 1, depth, rows, lanes), shape(depth, rows, lanes)]
        + [shape(rows, lanes)] * 2
        + [shape(depth, lanes)] * 2
        + [shape(rows, lanes)] * 2,
        in_specs=[stack(count, 0), below_of(count, 0), above_of(count, 0), tops, tops, edges, edges, sides, sides],
        out_specs=[stack(count, 0), planes, side, side, edge, edge, side, side],
        compiler_params=params(),
    )(gas_state, gas_state, gas_state, zlo, zhi, xlo, xhi, ylo, yhi)
    mix_halos = swap(mz_first, mz_last, mx_first, mx_last, my_first, my_last, 1)
    mix_below = pl.BlockSpec((1, rows, lanes), lambda i: (jnp.maximum(i * CHUNK - 1, 0), 0, 0))
    mix_above = pl.BlockSpec((1, rows, lanes), lambda i: (jnp.minimum((i + 1) * CHUNK, depth - 1), 0, 0))
    gas_next, local, ends = pl.pallas_call(
        energy_kernel,
        grid=(steps,),
        out_shape=[
            shape(count + 1, depth, rows, lanes),
            shape(depth * rows, lanes),
            shape(2 * rows + 8, lanes),
        ],
        in_specs=[
            stack(2, 0), stack(1, count), below_of(1, count), above_of(1, count),
            planes, mix_below, mix_above, planes, side, side,
            fixed(*block_inverse.shape), fixed(*line_coupling.shape),
            tops, tops, edges, edges, sides, sides,
            side, side, edge, edge, side, side, ANY,
        ],
        out_specs=[stack(1, count), fixed(depth * rows, lanes), fixed(2 * rows + 8, lanes)],
        scratch_shapes=[pltpu.VMEM((depth * rows, lanes), F32)],
        input_output_aliases={24: 0},
        compiler_params=params(),
    )(
        gas_state, gas_state, gas_state, gas_state, mix, mix, mix, solids_temp, exchange_rate, column_flags,
        block_inverse, line_coupling, zlo, zhi, xlo, xhi, ylo, yhi, *mix_halos, gas_next,
    )
    slots = pl.pallas_call(
        share_kernel,
        out_shape=shape(segments, 2 * rows + 8, lanes),
        in_specs=[VMEM],
        out_specs=VMEM,
        scratch_shapes=[pltpu.SemaphoreType.DMA((segments,)), pltpu.SemaphoreType.DMA((segments,))],
        compiler_params=pltpu.CompilerParams(collective_id=2, has_side_effects=True),
    )(ends)
    solved = pl.pallas_call(
        finish_kernel,
        out_shape=shape(depth * rows, lanes),
        in_specs=[VMEM] * 3,
        out_specs=VMEM,
        compiler_params=params(),
    )(slots, local, block_inverse)
    return (gas_next, solved.reshape(depth, rows, lanes))


def solution(mesh):
    in_specs = (
        P(None, "seg", "gx", "gy"),
        P("seg", "gx", "gy"),
        P("gx", "gy"),
        P("gx", "gy"),
        P("seg", None),
        P("seg", None),
    )
    out_specs = (P(None, "seg", "gx", "gy"), P("seg", "gx", "gy"))
    return jax.shard_map(body, mesh=mesh, in_specs=in_specs, out_specs=out_specs, check_vma=False)
```

time: 204 us -> 74.1 us (0.36)
  other arithmetic: 87.1 us -> 0 us
  Pallas kernels: 0 us -> 52 us
  starting transfers between devices: 39.8 us -> 0 us
  local copies, waits for them, and re-layouts: 45.7 us -> 20.2 us
  blocking collectives: 19.4 us -> 0 us
  waiting for transfers between devices: 6.94 us -> 0 us
  matrix products: 2.19 us -> 0 us
    pallas_call x0 -> x7, Pallas kernels: none -> 52 us  [the longest x2 16.1 us: swap(): pl.pallas_call(swap_gas_kernel, out_shape=[shape(*face.shape) for face in...]
    reduce_sum x1 -> x0, other arithmetic: 48.4 us -> none  [body(): mix = 0.5 * jnp.sum(species_new, axis=0)]
    ppermute x16 -> x0, starting transfers between devices: 39.8 us -> none  [the longest x8 28.9 us: with_halo(): lax.ppermute(lax.slice_in_dim(block, block.shape[dim] - width, None, axis...]
    concatenate x3 -> x0, other arithmetic: 11.3 us -> none  [the longest x1 7.02 us: body(): gas_next = jnp.concatenate([species_new, heat_new[None]], axis=0)]
    slice x17 -> x0, local copies, waits for them, and re-layouts: 10.8 us -> none  [the longest x8 4.69 us: reduced_inverse(): pivot_inv = inverse[step] / matrix[step, step]]
    broadcast_in_dim x16 -> x0, other arithmetic: 10.4 us -> none  [the longest x8 5.23 us: reduced_inverse(): inverse = jnp.where(is_pivot[:, None], pivot_inv[None], inverse)]
    ppermute x4 -> x0, local copies, waits for them, and re-layouts: 10.4 us -> none  [the longest x2 5.54 us: with_halo(): lax.ppermute(lax.slice_in_dim(block, block.shape[dim] - width, None, axis...]
    unnamed x1 -> x0, blocking collectives: 9.74 us -> none
  transfers between devices with their start and end apart: 16 -> 0, of which waited for: 4 -> 0; matrix products, arithmetic and copies ran while one was open for 54% -> 0% of each run, Pallas kernels for 0% -> 0%
where the time goes in v1:
time: 74.1 us; the launch traced here: 73 us
  Pallas kernels  52 us (70%)
  local copies, waits for them, and re-layouts  20.2 us (27%)
  between operations  0.86 us (1%)
    unnamed x72, local copies, waits for them, and re-layouts  18.7 us
    pallas_call x2, Pallas kernels, swap(): pl.pallas_call(swap_gas_kernel, out_shape=[shape(*face.shape) for face in...  16.1 us
    pallas_call x1, Pallas kernels, body(): pl.pallas_call(species_kernel, grid=(steps,), out_shape=[shape(count + 1,...  15.2 us
    pallas_call x1, Pallas kernels, body(): pl.pallas_call(energy_kernel, grid=(steps,), out_shape=[shape(count + 1,...  6.89 us
    pallas_call x1, Pallas kernels, body(): pl.pallas_call(share_kernel, out_shape=shape(segments, 2 * rows + 8, lane...  6.35 us
    pallas_call x1, Pallas kernels, body(): pl.pallas_call(pack_kernel, grid=(steps,), out_shape=[shape(fields, depth...  6.32 us
    squeeze x1, local copies, waits for them, and re-layouts, body(): gas_state[:, depth - 1]  1.5 us

profile of v1, /device:TPU:0, one launch (start us, length us, event | category | flops | bytes accessed | tf_op | source)
XLA Modules:
  0.0 73.0 jit_solution(16622856450924323115)
XLA Ops:
  0.6 1.5 %slice_bitcast_fusion = (f32[7,16,128]{2,1,0:T(8,128)}, f32[7,16,128]{2,1,0:T(8,128)}) fusion(f32[7,96,16,128]{3,2,1,0:T(8,128)} %heat_after.1), kind=kLoop, calls=%fused_computation | loop fusion | bytes 229376 | tf_op jit(solution)/shard_map/squeeze | solution.py:384
  2.1 0.0 copy-start
  2.1 1.1 %copy-done = f32[96,16,128]{2,1,0:T(8,128)S(1)} copy-done((f32[96,16,128]{2,1,0:T(8,128)S(1)}, f32[96,16,128]{2,1,0:T(8,128)}, u32[]{:S(2)}) %copy-start) | copy-done | bytes 786456
  3.3 6.3 %shard_map.77 = (f32[8,96,128]{2,1,0:T(8,128)S(1)}, f32[8,96,128]{2,1,0:T(8,128)S(1)}, f32[8,16,128]{2,1,0:T(8,128)S(1)}, f32[8,16,128]{2,1,0:T(8,128)S(1)}) custom-call(f32[7,96,16,128]{3,2,1,0:T(8,128)} %heat_after.1, f32[96,16,128]{2,1,0:T(8,128)S(1)} %copy-done), custom_call_target="tpu_custom_call" | custom-call | tf_op jit(solution)/shard_map/pallas_call | solution.py:375
  9.6 0.0 copy-start.6
  9.6 0.7 %copy-done.6 = f32[8,96,128]{2,1,0:T(8,128)} copy-done((f32[8,96,128]{2,1,0:T(8,128)}, f32[8,96,128]{2,1,0:T(8,128)S(1)}, u32[]{:S(2)}) %copy-start.6) | copy-done | bytes 393240
  10.3 0.0 copy-start.7
  10.3 0.7 %copy-done.7 = f32[8,96,128]{2,1,0:T(8,128)} copy-done((f32[8,96,128]{2,1,0:T(8,128)}, f32[8,96,128]{2,1,0:T(8,128)S(1)}, u32[]{:S(2)}) %copy-start.7) | copy-done | bytes 393240
  11.1 0.0 copy-start.18
  11.1 0.6 copy-done.18
  11.7 0.0 copy-start.19
  11.7 0.6 copy-done.19
  12.3 9.6 %shard_map.78 = (f32[7,16,128]{2,1,0:T(8,128)}, f32[7,16,128]{2,1,0:T(8,128)}, f32[8,96,128]{2,1,0:T(8,128)}, f32[8,96,128]{2,1,0:T(8,128)}, f32[8,16,128]{2,1,0:T(8,128)}, /*index=5*/f32[8,16,128]{2,1,0:T(8,128)}) custom-call(f32[7,16,128]{2,1,0:T(8,128)} %get-tuple-element.57.z_first, f32[7,16,128]{2,1,0:T(8,128)} %get-tuple-element.56.z_last, ...), custom_call_target="tpu_custom_call" | custom-call | tf_op jit(solution)/shard_map/pallas_call | solution.py:142
  22.0 0.0 copy-start.2
  22.0 1.0 %copy-done.2 = f32[8,96,128]{2,1,0:T(8,128)S(1)} copy-done((f32[8,96,128]{2,1,0:T(8,128)S(1)}, f32[8,96,128]{2,1,0:T(8,128)}, u32[]{:S(2)}) %copy-start.2) | copy-done | bytes 393240
  23.0 0.0 copy-start.4
  23.0 1.0 %copy-done.4 = f32[8,96,128]{2,1,0:T(8,128)S(1)} copy-done((f32[8,96,128]{2,1,0:T(8,128)S(1)}, f32[8,96,128]{2,1,0:T(8,128)}, u32[]{:S(2)}) %copy-start.4) | copy-done | bytes 393240
  24.0 0.0 copy-start.9
  24.0 0.8 %copy-done.9 = f32[8,16,128]{2,1,0:T(8,128)S(1)} copy-done((f32[8,16,128]{2,1,0:T(8,128)S(1)}, f32[8,16,128]{2,1,0:T(8,128)}, u32[]{:S(2)}) %copy-start.9) | copy-done | bytes 65560
  24.8 0.0 copy-start.11
  24.8 0.8 %copy-done.11 = f32[8,16,128]{2,1,0:T(8,128)S(1)} copy-done((f32[8,16,128]{2,1,0:T(8,128)S(1)}, f32[8,16,128]{2,1,0:T(8,128)}, u32[]{:S(2)}) %copy-start.11) | copy-done | bytes 65560
  25.6 0.0 copy-start.13
  25.7 0.8 %copy-done.13 = f32[7,16,128]{2,1,0:T(8,128)S(1)} copy-done((f32[7,16,128]{2,1,0:T(8,128)S(1)}, f32[7,16,128]{2,1,0:T(8,128)}, u32[]{:S(2)}) %copy-start.13) | copy-done | bytes 57368
  26.5 0.0 copy-start.15
  26.5 0.8 %copy-done.15 = f32[7,16,128]{2,1,0:T(8,128)S(1)} copy-done((f32[7,16,128]{2,1,0:T(8,128)S(1)}, f32[7,16,128]{2,1,0:T(8,128)}, u32[]{:S(2)}) %copy-start.15) | copy-done | bytes 57368
  27.3 0.0 copy-start.12
  27.3 0.0 copy-start.14
  27.3 0.0 copy-start.16
  27.3 0.0 copy-start.17
  27.3 0.0 copy-start.25
  27.4 0.0 copy-start.26
  27.4 0.0 copy-start.35
  27.4 15.2 %shard_map.79 = (f32[7,96,16,128]{3,2,1,0:T(8,128)}, f32[96,16,128]{2,1,0:T(8,128)S(1)}, f32[16,128]{1,0:T(8,128)S(1)}, f32[16,128]{1,0:T(8,128)S(1)}, f32[96,12...) custom-call(f32[7,96,16,128]{3,2,1,0:T(8,128)} %heat_after.1, ...), custom_call_target="tpu_custom_call" | custom-call | tf_op jit(solution)/shard_map/pallas_call | solution.py:386
  42.6 0.6 copy-done.22
  43.2 0.6 copy-done.23
  43.8 0.6 copy-done.32
  44.4 0.6 copy-done.33
  45.0 0.6 copy-done.34
  45.6 0.6 copy-done.31
  46.2 6.4 %shard_map.80 = (f32[16,128]{1,0:T(8,128)}, f32[16,128]{1,0:T(8,128)}, f32[96,128]{1,0:T(8,128)}, f32[96,128]{1,0:T(8,128)}, f32[16,128]{1,0:T(8,128)}, /*index=5*/f32[16,128]{1,0:T(8,128)}) custom-call(f32[16,128]{1,0:T(8,128)} %copy-done.31, f32[16,128]{1,0:T(8,128)} %copy-done.32, f32[96,128]{1,0:T(8,128)} %copy-done.22, f32[96,128]{1,0:T(8,128)} %copy-done.23, ...), custom_call_target="tpu_custom_call" | custom-call | tf_op jit(solution)/shard_map/pallas_call | solution.py:142
  52.6 0.0 copy-done.1
  52.6 0.0 copy-done.3
  52.6 0.0 copy-done.5
  52.7 0.0 copy-done.10
  52.7 0.0 copy-done.12
  52.7 0.0 copy-done.14
  52.7 0.0 copy-done.16
  52.7 0.0 copy-done.17
  52.7 0.0 copy-done.25
  52.7 0.0 copy-done.26
  52.7 0.0 copy-done.35
  52.7 0.0 copy-start.20
  52.7 0.8 %copy-done.20 = f32[96,128]{1,0:T(8,128)S(1)} copy-done((f32[96,128]{1,0:T(8,128)S(1)}, f32[96,128]{1,0:T(8,128)}, u32[]{:S(2)}) %copy-start.20) | copy-done | bytes 49176
  53.5 0.8 %copy-done.21 = f32[96,128]{1,0:T(8,128)S(1)} copy-done((f32[96,128]{1,0:T(8,128)S(1)}, f32[96,128]{1,0:T(8,128)}, u32[]{:S(2)}) %copy-start.21) | copy-done | bytes 49176
  54.3 0.7 copy-done.27
  55.0 0.7 copy-done.28
  55.7 0.7 copy-done.29
  56.4 0.7 copy-done.30
  57.1 6.9 %shard_map.81 = (f32[7,96,16,128]{3,2,1,0:T(8,128)}, f32[1536,128]{1,0:T(8,128)S(1)}, f32[40,128]{1,0:T(8,128)S(1)}) custom-call(f32[7,96,16,128]{3,2,1,0:T(8,128)} %heat_after.1, f32[7,96,16,128]{3,2,1,0:T(8,128)} %heat_after.1, f32[7,96,16,128]{3,2,1,0:T(8,128)} %heat_after.1, f32[7,96,16,128]{3,2,1,0:T(8,128)} %heat_after.1, ...), custom_call_target="tpu_custom_call", output_to_operand_aliasing={{0}: (24, {})} | custom-call | tf_op jit(solution)/shard_map/pallas_call | solution.py:400
  64.0 0.6 copy-done.24
  64.6 6.4 %shard_map.82.slots = f32[4,40,128]{2,1,0:T(8,128)} custom-call(f32[40,128]{1,0:T(8,128)} %copy-done.24), custom_call_target="tpu_custom_call" | custom-call | tf_op jit(solution)/shard_map/pallas_call | solution.py:423
  71.0 0.0 copy-start.8
  71.0 0.9 %copy-done.8 = f32[4,40,128]{2,1,0:T(8,128)S(1)} copy-done((f32[4,40,128]{2,1,0:T(8,128)S(1)}, f32[4,40,128]{2,1,0:T(8,128)}, u32[]{:S(2)}) %copy-start.8) | copy-done | bytes 81944
  71.9 1.1 %shard_map.83 = f32[1536,128]{1,0:T(8,128)} custom-call(f32[4,40,128]{2,1,0:T(8,128)S(1)} %copy-done.8, f32[1536,128]{1,0:T(8,128)S(1)} %get-tuple-element.55.local, f32[96,96]{1,0:T(8,128)S(1)} %copy-done.17), custom_call_target="tpu_custom_call" | custom-call | tf_op jit(solution)/shard_map/pallas_call | solution.py:431
  (16 shorter events, 0.0 us)
Async XLA Ops:
  2.1 1.1 %copy-start = (f32[96,16,128]{2,1,0:T(8,128)S(1)}, f32[96,16,128]{2,1,0:T(8,128)}, u32[]{:S(2)}) copy-start(f32[96,16,128]{2,1,0:T(8,128)} %temp.3) | copy-start | bytes 2359300
  9.6 0.7 %copy-start.6 = (f32[8,96,128]{2,1,0:T(8,128)}, f32[8,96,128]{2,1,0:T(8,128)S(1)}, u32[]{:S(2)}) copy-start(f32[8,96,128]{2,1,0:T(8,128)S(1)} %get-tuple-element.29.x_first) | copy-start | bytes 1179652
  10.3 0.7 %copy-start.7 = (f32[8,96,128]{2,1,0:T(8,128)}, f32[8,96,128]{2,1,0:T(8,128)S(1)}, u32[]{:S(2)}) copy-start(f32[8,96,128]{2,1,0:T(8,128)S(1)} %get-tuple-element.30.x_last) | copy-start | bytes 1179652
  11.1 0.6 copy-start.18
  11.7 0.6 copy-start.19
  22.0 1.0 %copy-start.2 = (f32[8,96,128]{2,1,0:T(8,128)S(1)}, f32[8,96,128]{2,1,0:T(8,128)}, u32[]{:S(2)}) copy-start(f32[8,96,128]{2,1,0:T(8,128)} %get-tuple-element.35.xlo) | copy-start | bytes 1179652
  23.0 1.0 %copy-start.4 = (f32[8,96,128]{2,1,0:T(8,128)S(1)}, f32[8,96,128]{2,1,0:T(8,128)}, u32[]{:S(2)}) copy-start(f32[8,96,128]{2,1,0:T(8,128)} %get-tuple-element.36.xhi) | copy-start | bytes 1179652
  24.0 0.8 %copy-start.9 = (f32[8,16,128]{2,1,0:T(8,128)S(1)}, f32[8,16,128]{2,1,0:T(8,128)}, u32[]{:S(2)}) copy-start(f32[8,16,128]{2,1,0:T(8,128)} %get-tuple-element.37.ylo) | copy-start | bytes 196612
  24.8 0.8 %copy-start.11 = (f32[8,16,128]{2,1,0:T(8,128)S(1)}, f32[8,16,128]{2,1,0:T(8,128)}, u32[]{:S(2)}) copy-start(f32[8,16,128]{2,1,0:T(8,128)} %get-tuple-element.38.yhi) | copy-start | bytes 196612
  25.6 0.8 %copy-start.13 = (f32[7,16,128]{2,1,0:T(8,128)S(1)}, f32[7,16,128]{2,1,0:T(8,128)}, u32[]{:S(2)}) copy-start(f32[7,16,128]{2,1,0:T(8,128)} %get-tuple-element.33.zlo) | copy-start | bytes 172036
  26.5 0.8 %copy-start.15 = (f32[7,16,128]{2,1,0:T(8,128)S(1)}, f32[7,16,128]{2,1,0:T(8,128)}, u32[]{:S(2)}) copy-start(f32[7,16,128]{2,1,0:T(8,128)} %get-tuple-element.34.zhi) | copy-start | bytes 172036
  27.3 25.3 %copy-start.1 = (f32[96,16,128]{2,1,0:T(8,128)S(1)}, f32[96,16,128]{2,1,0:T(8,128)}, u32[]{:S(2)}) copy-start(f32[96,16,128]{2,1,0:T(8,128)} %temp.3) | copy-start | bytes 2359300
  27.3 25.3 %copy-start.3 = (f32[8,96,128]{2,1,0:T(8,128)S(1)}, f32[8,96,128]{2,1,0:T(8,128)}, u32[]{:S(2)}) copy-start(f32[8,96,128]{2,1,0:T(8,128)} %get-tuple-element.35.xlo) | copy-start | bytes 1179652
  27.3 25.4 %copy-start.5 = (f32[8,96,128]{2,1,0:T(8,128)S(1)}, f32[8,96,128]{2,1,0:T(8,128)}, u32[]{:S(2)}) copy-start(f32[8,96,128]{2,1,0:T(8,128)} %get-tuple-element.36.xhi) | copy-start | bytes 1179652
  27.3 25.4 %copy-start.10 = (f32[8,16,128]{2,1,0:T(8,128)S(1)}, f32[8,16,128]{2,1,0:T(8,128)}, u32[]{:S(2)}) copy-start(f32[8,16,128]{2,1,0:T(8,128)} %get-tuple-element.37.ylo) | copy-start | bytes 196612
  27.3 25.4 %copy-start.12 = (f32[8,16,128]{2,1,0:T(8,128)S(1)}, f32[8,16,128]{2,1,0:T(8,128)}, u32[]{:S(2)}) copy-start(f32[8,16,128]{2,1,0:T(8,128)} %get-tuple-element.38.yhi) | copy-start | bytes 196612
  27.3 25.4 %copy-start.14 = (f32[7,16,128]{2,1,0:T(8,128)S(1)}, f32[7,16,128]{2,1,0:T(8,128)}, u32[]{:S(2)}) copy-start(f32[7,16,128]{2,1,0:T(8,128)} %get-tuple-element.33.zlo) | copy-start | bytes 172036
  27.3 25.4 %copy-start.16 = (f32[7,16,128]{2,1,0:T(8,128)S(1)}, f32[7,16,128]{2,1,0:T(8,128)}, u32[]{:S(2)}) copy-start(f32[7,16,128]{2,1,0:T(8,128)} %get-tuple-element.34.zhi) | copy-start | bytes 172036
  27.3 25.4 %copy-start.17 = (f32[96,96]{1,0:T(8,128)S(1)}, f32[96,96]{1,0:T(8,128)}, u32[]{:S(2)}) copy-start(f32[96,96]{1,0:T(8,128)} %inverse.3) | copy-start | bytes 110596
  27.3 25.4 %copy-start.25 = (f32[16,128]{1,0:T(8,128)S(1)}, f32[16,128]{1,0:T(8,128)}, u32[]{:S(2)}) copy-start(f32[16,128]{1,0:T(8,128)} %exchange.1) | copy-start | bytes 24580
  27.4 25.4 %copy-start.26 = (s32[16,128]{1,0:T(8,128)S(1)}, s32[16,128]{1,0:T(8,128)}, u32[]{:S(2)}) copy-start(s32[16,128]{1,0:T(8,128)} %flags.1) | copy-start | bytes 24580
  27.4 25.4 %copy-start.35 = (f32[1,2]{1,0:T(1,128)S(1)}, f32[1,2]{1,0:T(1,128)}, u32[]{:S(2)}) copy-start(f32[1,2]{1,0:T(1,128)} %coupling.1) | copy-start | bytes 28
  42.6 0.6 copy-start.22
  43.2 0.6 copy-start.23
  43.8 0.6 copy-start.32
  44.4 0.6 copy-start.33
  45.0 0.6 copy-start.34
  45.6 0.6 copy-start.31
  52.7 0.8 %copy-start.20 = (f32[96,128]{1,0:T(8,128)S(1)}, f32[96,128]{1,0:T(8,128)}, u32[]{:S(2)}) copy-start(f32[96,128]{1,0:T(8,128)} %get-tuple-element.48.mxlo) | copy-start | bytes 147460
  53.5 0.8 %copy-start.21 = (f32[96,128]{1,0:T(8,128)S(1)}, f32[96,128]{1,0:T(8,128)}, u32[]{:S(2)}) copy-start(f32[96,128]{1,0:T(8,128)} %get-tuple-element.49.mxhi) | copy-start | bytes 147460
  54.3 0.7 copy-start.27
  55.0 0.7 copy-start.28
  55.7 0.7 copy-start.29
  56.4 0.7 copy-start.30
  64.0 0.6 copy-start.24
  71.0 0.9 %copy-start.8 = (f32[4,40,128]{2,1,0:T(8,128)S(1)}, f32[4,40,128]{2,1,0:T(8,128)}, u32[]{:S(2)}) copy-start(f32[4,40,128]{2,1,0:T(8,128)} %shard_map.82.slots) | copy-start | bytes 245764

commit v2 on v1

--- a/solution.py
+++ b/solution.py
@@ -19,7 +19,6 @@
 
 
 MESH = pl.DeviceIdType.MESH
-VMEM = pl.BlockSpec(memory_space=pltpu.VMEM)
 ANY = pl.BlockSpec(memory_space=pl.ANY)
 F32 = jnp.float32
 CHUNK = 16
@@ -30,7 +29,7 @@
 
 
 def params():
-    return pltpu.CompilerParams(vmem_limit_bytes=48 * 1024 * 1024)
+    return pltpu.CompilerParams(vmem_limit_bytes=63 * 1024 * 1024)
 
 
 def iotas(rows, lanes):
@@ -80,7 +79,7 @@
         y_last[field] = last
 
 
-def swap_faces(axes, send_sem, recv_sem):
+def swap_faces(axes, blank, zero_sem, send_sem, recv_sem):
     barrier = pltpu.get_barrier_semaphore()
     places = []
     for name, *_ in axes:
@@ -108,49 +107,66 @@
     for to_up, to_down, down, up, low, high in plan:
         pl.when(up)(to_up.start)
         pl.when(down)(to_down.start)
-    for to_up, to_down, down, up, low, high in plan:
-
-        @pl.when(jnp.logical_not(down))
-        def _(low=low):
-            low[...] = jnp.zeros(low.shape, F32)
-
-        @pl.when(jnp.logical_not(up))
-        def _(high=high):
-            high[...] = jnp.zeros(high.shape, F32)
-
+    blank[...] = jnp.zeros(blank.shape, F32)
+    fills = []
+    for index, (_, _, down, up, low, high) in enumerate(plan):
+        for side, (exists, halo) in enumerate(((down, low), (up, high))):
+            part = blank
+            if len(halo.shape) == 2:
+                part = blank.at[0, pl.ds(0, halo.shape[0])]
+            else:
+                part = blank.at[pl.ds(0, halo.shape[0]), pl.ds(0, halo.shape[1])]
+            fill = pltpu.make_async_copy(part, halo, zero_sem.at[2 * index + side])
+            fills.append((jnp.logical_not(exists), fill))
+    for missing, fill in fills:
+        pl.when(missing)(fill.start)
     for to_up, to_down, down, up, low, high in plan:
         pl.when(up)(to_up.wait_send)
         pl.when(down)(to_down.wait_send)
         pl.when(down)(to_up.wait_recv)
         pl.when(up)(to_down.wait_recv)
-
-
-def swap_gas_kernel(z_first, z_last, x_first, x_last, y_first, y_last, zlo, zhi, xlo, xhi, ylo, yhi, send_sem, recv_sem):
+    for missing, fill in fills:
+        pl.when(missing)(fill.wait)
+
+
+def swap_kernel(
+    field, x_first, x_last, y_first, y_last, zlo, zhi, xlo, xhi, ylo, yhi, blank, zero_sem, send_sem, recv_sem
+):
+    if len(field.shape) == 4:
+        z_first, z_last = field.at[:, 0], field.at[:, field.shape[1] - 1]
+    else:
+        z_first, z_last = field.at[0], field.at[field.shape[0] - 1]
     swap_faces(
         (
             ("gx", x_first, x_last, xlo, xhi),
             ("seg", z_first, z_last, zlo, zhi),
             ("gy", y_first, y_last, ylo, yhi),
         ),
+        blank,
+        zero_sem,
         send_sem,
         recv_sem,
     )
 
 
-def swap(z_first, z_last, x_first, x_last, y_first, y_last, ident):
-    faces = (z_first, z_last, x_first, x_last, y_first, y_last)
+def swap(field, x_first, x_last, y_first, y_last, ident):
+    top = shape(*field.shape[:-3], *field.shape[-2:])
+    side = shape(*x_first.shape)
+    edge = shape(*y_first.shape)
+    blank = (1,) * (3 - x_first.ndim) + x_first.shape
+    sems = pltpu.SemaphoreType.DMA((6,))
     return pl.pallas_call(
-        swap_gas_kernel,
-        out_shape=[shape(*face.shape) for face in faces],
-        in_specs=[VMEM] * 6,
-        out_specs=[VMEM] * 6,
-        scratch_shapes=[pltpu.SemaphoreType.DMA((6,)), pltpu.SemaphoreType.DMA((6,))],
-        compiler_params=pltpu.CompilerParams(collective_id=ident, has_side_effects=True),
-    )(*faces)
+        swap_kernel,
+        out_shape=[top, top, side, side, edge, edge],
+        in_specs=[ANY] * 5,
+        out_specs=[ANY] * 6,
+        scratch_shapes=[pltpu.VMEM(blank, F32), sems, sems, sems],
+        compiler_params=pltpu.CompilerParams(collective_id=ident, has_side_effects=True, vmem_limit_bytes=63 * 1024 * 1024),
+    )(field, x_first, x_last, y_first, y_last)
 
 
 def species_kernel(
-    gas, before, after, zlo, zhi, xlo, xhi, ylo, yhi, new, mix_out, z_first, z_last, x_first, x_last, y_first, y_last
+    gas, before, after, zlo, zhi, xlo, xhi, ylo, yhi, new, mix_out, x_first, x_last, y_first, y_last
 ):
     step, steps = pl.program_id(0), pl.num_programs(0)
     count, depth, rows, lanes = gas.shape
@@ -189,18 +205,6 @@
         last = pack_columns(last, mix, z, lane, True)
         x_first[k : k + 1] = mix[0:1]
         x_last[k : k + 1] = mix[rows - 1 : rows]
-        if k == 0:
-
-            @pl.when(at_bottom)
-            def _(mix=mix):
-                z_first[...] = mix
-
-        if k == depth - 1:
-
-            @pl.when(at_top)
-            def _(mix=mix):
-                z_last[...] = mix
-
     y_first[...] = first
     y_last[...] = last
 
@@ -277,7 +281,7 @@
         ends[2 * rows + 6 : 2 * rows + 8] = jnp.zeros((2, lanes), F32)
 
 
-def share_kernel(ends, slots, send_sem, recv_sem):
+def share_kernel(ends, slots, own_sem, send_sem, recv_sem):
     here, count = lax.axis_index("seg"), lax.axis_size("seg")
     barrier = pltpu.get_barrier_semaphore()
     for step in range(1, count):
@@ -292,7 +296,9 @@
     ]
     for copy in copies:
         copy.start()
-    slots[0] = ends[...]
+    own = pltpu.make_async_copy(ends, slots.at[0], own_sem)
+    own.start()
+    own.wait()
     for copy in copies:
         copy.wait()
 
@@ -300,7 +306,7 @@
 def finish_kernel(slots, local, inverse, out):
     count, total_rows, lanes = slots.shape
     rows = (total_rows - 8) // 2
-    size = inverse.shape[0]
+    size, width = inverse.shape
     here = lax.axis_index("seg")
     held = [slots[lax.rem(here - s + count, count)] for s in range(count)]
     p_lines, q_lines = [], []
@@ -339,7 +345,7 @@
     p_near = mine[2 * rows + 5 : 2 * rows + 6] * p_near
     for z in range(size):
         low = jnp.broadcast_to(inverse[z : z + 1, 0:1], (1, lanes))
-        high = jnp.broadcast_to(inverse[z : z + 1, size - 1 : size], (1, lanes))
+        high = jnp.broadcast_to(inverse[z : z + 1, width - 1 : width], (1, lanes))
         block = slice(z * rows, (z + 1) * rows)
         out[block] = local[block] + q_near * low + p_near * high
 
@@ -381,20 +387,19 @@
         compiler_params=params(),
     )(gas_state, solids_temp)
     zlo, zhi, xlo, xhi, ylo, yhi = swap(
-        gas_state[:, 0], gas_state[:, depth - 1], x_first, x_last, y_first, y_last, 0
+        gas_state, x_first, x_last, y_first, y_last, 0
     )
-    gas_next, mix, mz_first, mz_last, mx_first, mx_last, my_first, my_last = pl.pallas_call(
+    gas_next, mix, mx_first, mx_last, my_first, my_last = pl.pallas_call(
         species_kernel,
         grid=(steps,),
         out_shape=[shape(count + 1, depth, rows, lanes), shape(depth, rows, lanes)]
-        + [shape(rows, lanes)] * 2
         + [shape(depth, lanes)] * 2
         + [shape(rows, lanes)] * 2,
         in_specs=[stack(count, 0), below_of(count, 0), above_of(count, 0), tops, tops, edges, edges, sides, sides],
-        out_specs=[stack(count, 0), planes, side, side, edge, edge, side, side],
+        out_specs=[stack(count, 0), planes, edge, edge, side, side],
         compiler_params=params(),
     )(gas_state, gas_state, gas_state, zlo, zhi, xlo, xhi, ylo, yhi)
-    mix_halos = swap(mz_first, mz_last, mx_first, mx_last, my_first, my_last, 1)
+    mix_halos = swap(mix, mx_first, mx_last, my_first, my_last, 1)
     mix_below = pl.BlockSpec((1, rows, lanes), lambda i: (jnp.maximum(i * CHUNK - 1, 0), 0, 0))
     mix_above = pl.BlockSpec((1, rows, lanes), lambda i: (jnp.minimum((i + 1) * CHUNK, depth - 1), 0, 0))
     gas_next, local, ends = pl.pallas_call(
@@ -423,16 +428,22 @@
     slots = pl.pallas_call(
         share_kernel,
         out_shape=shape(segments, 2 * rows + 8, lanes),
-        in_specs=[VMEM],
-        out_specs=VMEM,
-        scratch_shapes=[pltpu.SemaphoreType.DMA((segments,)), pltpu.SemaphoreType.DMA((segments,))],
-        compiler_params=pltpu.CompilerParams(collective_id=2, has_side_effects=True),
+        in_specs=[ANY],
+        out_specs=ANY,
+        scratch_shapes=[pltpu.SemaphoreType.DMA(()), pltpu.SemaphoreType.DMA((segments,)), pltpu.SemaphoreType.DMA((segments,))],
+        compiler_params=pltpu.CompilerParams(collective_id=2, has_side_effects=True, vmem_limit_bytes=63 * 1024 * 1024),
     )(ends)
+    part = 2 * CHUNK
     solved = pl.pallas_call(
         finish_kernel,
         out_shape=shape(depth * rows, lanes),
-        in_specs=[VMEM] * 3,
-        out_specs=VMEM,
+        grid=(depth // part,),
+        in_specs=[
+            fixed(segments, 2 * rows + 8, lanes),
+            pl.BlockSpec((part * rows, lanes), lambda i: (i, 0)),
+            pl.BlockSpec((part, depth), lambda i: (i, 0)),
+        ],
+        out_specs=pl.BlockSpec((part * rows, lanes), lambda i: (i, 0)),
         compiler_params=params(),
     )(slots, local, block_inverse)
     return (gas_next, solved.reshape(depth, rows, lanes))

time: 74.1 us -> 52.9 us (0.71)
  local copies, waits for them, and re-layouts: 20.2 us -> 0 us
    unnamed x72 -> x0, local copies, waits for them, and re-layouts: 18.7 us -> none
    squeeze x1 -> x0, local copies, waits for them, and re-layouts: 1.5 us -> none  [body(): gas_state[:, depth - 1]]
    pallas_call x1, Pallas kernels: 6.89 us -> 7.99 us  [body(): pl.pallas_call(energy_kernel, grid=(steps,), out_shape=[shape(count + 1,...]
    pallas_call x1, Pallas kernels: 6.35 us -> 5.37 us  [body(): pl.pallas_call(share_kernel, out_shape=shape(segments, 2 * rows + 8, lane...]
    pallas_call x3, Pallas kernels: 17.2 us -> 16.4 us  [the longest x2 13.3 us: swap(): pl.pallas_call(swap_kernel, out_shape=[top, top, side, side, edge, edge],...]
    pallas_call x1, Pallas kernels: 6.32 us -> 7.11 us  [body(): pl.pallas_call(pack_kernel, grid=(steps,), out_shape=[shape(fields, depth...]
where the time goes in v2:
time: 52.9 us; the launch traced here: 52.4 us
  Pallas kernels  51.8 us (98%)
  between operations  0.67 us (1%)
    pallas_call x1, Pallas kernels, body(): pl.pallas_call(species_kernel, grid=(steps,), out_shape=[shape(count + 1,...  14.9 us
    pallas_call x2, Pallas kernels, swap(): pl.pallas_call(swap_kernel, out_shape=[top, top, side, side, edge, edge],...  13.3 us
    pallas_call x1, Pallas kernels, body(): pl.pallas_call(energy_kernel, grid=(steps,), out_shape=[shape(count + 1,...  7.99 us
    pallas_call x1, Pallas kernels, body(): pl.pallas_call(pack_kernel, grid=(steps,), out_shape=[shape(fields, depth...  7.11 us
    pallas_call x1, Pallas kernels, body(): pl.pallas_call(share_kernel, out_shape=shape(segments, 2 * rows + 8, lane...  5.37 us
    pallas_call x1, Pallas kernels, body(): pl.pallas_call(finish_kernel, out_shape=shape(depth * rows, lanes), grid=...  3.09 us

profile of v2, /device:TPU:0, one launch (start us, length us, event | category | flops | bytes accessed | tf_op | source)
XLA Modules:
  0.0 52.4 jit_solution(15703512987209709377)
XLA Ops:
  0.6 7.1 %shard_map.77 = (f32[8,96,128]{2,1,0:T(8,128)}, f32[8,96,128]{2,1,0:T(8,128)}, f32[8,16,128]{2,1,0:T(8,128)}, f32[8,16,128]{2,1,0:T(8,128)}) custom-call(f32[7,96,16,128]{3,2,1,0:T(8,128)} %heat_after.1, f32[96,16,128]{2,1,0:T(8,128)} %temp.3), custom_call_target="tpu_custom_call" | custom-call | tf_op jit(solution)/shard_map/pallas_call | solution.py:381
  7.7 7.9 %shard_map.78 = (f32[7,16,128]{2,1,0:T(8,128)}, f32[7,16,128]{2,1,0:T(8,128)}, f32[8,96,128]{2,1,0:T(8,128)}, f32[8,96,128]{2,1,0:T(8,128)}, f32[8,16,128]{2,1,0:T(8,128)}, /*index=5*/f32[8,16,128]{2,1,0:T(8,128)}) custom-call(f32[7,96,16,128]{3,2,1,0:T(8,128)} %heat_after.1, f32[8,96,128]{2,1,0:T(8,128)} %get-tuple-element.27.x_first, ...), custom_call_target="tpu_custom_call" | custom-call | tf_op jit(solution)/shard_map/pallas_call | solution.py:158
  15.7 14.9 %shard_map.79 = (f32[7,96,16,128]{3,2,1,0:T(8,128)}, f32[96,16,128]{2,1,0:T(8,128)}, f32[96,128]{1,0:T(8,128)}, f32[96,128]{1,0:T(8,128)}, f32[16,128]{1,0:T(8,128)}, /*index=5*/f32[16,128]{1,0:T(8,128)}) custom-call(f32[7,96,16,128]{3,2,1,0:T(8,128)} %heat_after.1, f32[7,96,16,128]{3,2,1,0:T(8,128)} %heat_after.1, f32[7,96,16,128]{3,2,1,0:T(8,128)} %heat_after.1, ...), custom_call_target="tpu_custom_call" | custom-call | tf_op jit(solution)/shard_map/pallas_call | solution.py:392
  30.6 5.3 %shard_map.80 = (f32[16,128]{1,0:T(8,128)}, f32[16,128]{1,0:T(8,128)}, f32[96,128]{1,0:T(8,128)}, f32[96,128]{1,0:T(8,128)}, f32[16,128]{1,0:T(8,128)}, /*index=5*/f32[16,128]{1,0:T(8,128)}) custom-call(f32[96,16,128]{2,1,0:T(8,128)} %get-tuple-element.37.field.mix.mix_before.mix_after, f32[96,128]{1,0:T(8,128)} %get-tuple-element.38.x_first, ...), custom_call_target="tpu_custom_call" | custom-call | tf_op jit(solution)/shard_map/pallas_call | solution.py:158
  36.0 8.0 %shard_map.81 = (f32[7,96,16,128]{3,2,1,0:T(8,128)}, f32[1536,128]{1,0:T(8,128)}, f32[40,128]{1,0:T(8,128)}) custom-call(f32[7,96,16,128]{3,2,1,0:T(8,128)} %heat_after.1, f32[7,96,16,128]{3,2,1,0:T(8,128)} %heat_after.1, f32[7,96,16,128]{3,2,1,0:T(8,128)} %heat_after.1, f32[7,96,16,128]{3,2,1,0:T(8,128)} %heat_after.1, ...), custom_call_target="tpu_custom_call", output_to_operand_aliasing={{0}: (24, {})} | custom-call | tf_op jit(solution)/shard_map/pallas_call | solution.py:405
  44.0 5.4 %shard_map.82.slots = f32[4,40,128]{2,1,0:T(8,128)} custom-call(f32[40,128]{1,0:T(8,128)} %get-tuple-element.50.ends), custom_call_target="tpu_custom_call" | custom-call | tf_op jit(solution)/shard_map/pallas_call | solution.py:428
  49.3 3.1 %shard_map.83 = f32[1536,128]{1,0:T(8,128)} custom-call(f32[4,40,128]{2,1,0:T(8,128)} %shard_map.82.slots, f32[1536,128]{1,0:T(8,128)} %get-tuple-element.51.local, f32[96,96]{1,0:T(8,128)} %inverse.3), custom_call_target="tpu_custom_call" | custom-call | tf_op jit(solution)/shard_map/pallas_call | solution.py:437

commit v3 on v2

--- a/solution.py
+++ b/solution.py
@@ -38,24 +38,40 @@
     return row, lane
 
 
-def pack_columns(packed, plane, z, lane, last):
+def pack_columns(packed, plane, k, lane):
     lanes = plane.shape[1]
-    moved = pltpu.roll(plane, lax.rem(z + 1, lanes) if last else z, 1)
-    return jnp.where(lane == z, moved, packed)
-
-
-def shifted(plane, row, lane, z, xlo, xhi, ylo, yhi):
+    moved = pltpu.roll(plane, 2 * k, 1) if k else plane
+    ours = (lane == 2 * k) | (lane == (2 * k - 1) % lanes)
+    return jnp.where(ours, moved, packed)
+
+
+def page_of(step, lanes):
+    per_page = lanes // (2 * CHUNK)
+    return step // per_page, lax.rem(step, per_page) * (2 * CHUNK)
+
+
+def merge_pages(low, high, lane):
+    lanes = low.shape[1]
+    return jnp.where(lane % 2 == 0, pltpu.roll(low, 1, 1), pltpu.roll(high, lanes - 1, 1))
+
+
+def chunk_halo(low, high, step, lane):
+    lanes = low.shape[1]
+    _, offset = page_of(step, lanes)
+    return pltpu.roll(merge_pages(low, high, lane), lax.rem(lanes - offset, lanes), 1)
+
+
+def shifted(plane, row, lane, k, xlo, xhi, halo):
     rows, lanes = plane.shape
     west = jnp.where(row == 0, xlo, pltpu.roll(plane, 1, 0))
     east = jnp.where(row == rows - 1, xhi, pltpu.roll(plane, rows - 1, 0))
-    low_col = pltpu.roll(ylo, lax.rem(lanes - z, lanes), 1)
-    high_col = pltpu.roll(yhi, lanes - 1 - z, 1)
-    south = jnp.where(lane == 0, low_col, pltpu.roll(plane, 1, 1))
-    north = jnp.where(lane == lanes - 1, high_col, pltpu.roll(plane, lanes - 1, 1))
+    column = pltpu.roll(halo, lanes - 2 * k, 1) if k else halo
+    south = jnp.where(lane == 0, column, pltpu.roll(plane, 1, 1))
+    north = jnp.where(lane == lanes - 1, column, pltpu.roll(plane, lanes - 1, 1))
     return west, east, south, north
 
 
-def pack_kernel(gas, temp, x_first, x_last, y_first, y_last):
+def pack_kernel(gas, temp, x_first, x_last, y_pair):
     step = pl.program_id(0)
     fields = gas.shape[0] + 1
     rows, lanes = gas.shape[2:]
@@ -63,23 +79,20 @@
 
     @pl.when(step == 0)
     def _():
-        y_first[...] = jnp.zeros_like(y_first)
-        y_last[...] = jnp.zeros_like(y_last)
-
+        y_pair[...] = jnp.zeros_like(y_pair)
+
+    page, offset = page_of(step, lanes)
     for field in range(fields):
-        first, last = y_first[field], y_last[field]
+        packed = jnp.zeros((rows, lanes), F32)
         for k in range(gas.shape[1]):
-            z = step * gas.shape[1] + k
             plane = gas[field, k] if field < fields - 1 else temp[k]
-            first = pack_columns(first, plane, z, lane, False)
-            last = pack_columns(last, plane, z, lane, True)
+            packed = pack_columns(packed, plane, k, lane)
             x_first[field, k : k + 1] = plane[0:1]
             x_last[field, k : k + 1] = plane[rows - 1 : rows]
-        y_first[field] = first
-        y_last[field] = last
-
-
-def swap_faces(axes, blank, zero_sem, send_sem, recv_sem):
+        y_pair[page, field] += pltpu.roll(packed, offset, 1)
+
+
+def swap_faces(axes, blanks, zero_sem, send_sem, recv_sem):
     barrier = pltpu.get_barrier_semaphore()
     places = []
     for name, *_ in axes:
@@ -107,16 +120,12 @@
     for to_up, to_down, down, up, low, high in plan:
         pl.when(up)(to_up.start)
         pl.when(down)(to_down.start)
-    blank[...] = jnp.zeros(blank.shape, F32)
+    for blank in blanks:
+        blank[...] = jnp.zeros(blank.shape, F32)
     fills = []
     for index, (_, _, down, up, low, high) in enumerate(plan):
         for side, (exists, halo) in enumerate(((down, low), (up, high))):
-            part = blank
-            if len(halo.shape) == 2:
-                part = blank.at[0, pl.ds(0, halo.shape[0])]
-            else:
-                part = blank.at[pl.ds(0, halo.shape[0]), pl.ds(0, halo.shape[1])]
-            fill = pltpu.make_async_copy(part, halo, zero_sem.at[2 * index + side])
+            fill = pltpu.make_async_copy(blanks[index], halo, zero_sem.at[2 * index + side])
             fills.append((jnp.logical_not(exists), fill))
     for missing, fill in fills:
         pl.when(missing)(fill.start)
@@ -130,7 +139,7 @@
 
 
 def swap_kernel(
-    field, x_first, x_last, y_first, y_last, zlo, zhi, xlo, xhi, ylo, yhi, blank, zero_sem, send_sem, recv_sem
+    field, x_first, x_last, y_pair, zlo, zhi, xlo, xhi, ylo, yhi, x_blank, z_blank, y_blank, zero_sem, send_sem, recv_sem
 ):
     if len(field.shape) == 4:
         z_first, z_last = field.at[:, 0], field.at[:, field.shape[1] - 1]
@@ -140,33 +149,32 @@
         (
             ("gx", x_first, x_last, xlo, xhi),
             ("seg", z_first, z_last, zlo, zhi),
-            ("gy", y_first, y_last, ylo, yhi),
+            ("gy", y_pair, y_pair, ylo, yhi),
         ),
-        blank,
+        (x_blank, z_blank, y_blank),
         zero_sem,
         send_sem,
         recv_sem,
     )
 
 
-def swap(field, x_first, x_last, y_first, y_last, ident):
+def swap(field, x_first, x_last, y_pair, ident):
     top = shape(*field.shape[:-3], *field.shape[-2:])
     side = shape(*x_first.shape)
-    edge = shape(*y_first.shape)
-    blank = (1,) * (3 - x_first.ndim) + x_first.shape
+    edge = shape(*y_pair.shape)
     sems = pltpu.SemaphoreType.DMA((6,))
     return pl.pallas_call(
         swap_kernel,
         out_shape=[top, top, side, side, edge, edge],
-        in_specs=[ANY] * 5,
+        in_specs=[ANY] * 4,
         out_specs=[ANY] * 6,
-        scratch_shapes=[pltpu.VMEM(blank, F32), sems, sems, sems],
+        scratch_shapes=[pltpu.VMEM(face.shape, F32) for face in (side, top, edge)] + [sems, sems, sems],
         compiler_params=pltpu.CompilerParams(collective_id=ident, has_side_effects=True, vmem_limit_bytes=63 * 1024 * 1024),
-    )(field, x_first, x_last, y_first, y_last)
+    )(field, x_first, x_last, y_pair)
 
 
 def species_kernel(
-    gas, before, after, zlo, zhi, xlo, xhi, ylo, yhi, new, mix_out, x_first, x_last, y_first, y_last
+    gas, before, after, zlo, zhi, xlo, xhi, ylo, yhi, new, mix_out, x_first, x_last, y_pair
 ):
     step, steps = pl.program_id(0), pl.num_programs(0)
     count, depth, rows, lanes = gas.shape
@@ -175,12 +183,12 @@
 
     @pl.when(step == 0)
     def _():
-        y_first[...] = jnp.zeros_like(y_first)
-        y_last[...] = jnp.zeros_like(y_last)
-
-    first, last = y_first[...], y_last[...]
+        y_pair[...] = jnp.zeros_like(y_pair)
+
+    page, offset = page_of(step, lanes)
+    packed = jnp.zeros((rows, lanes), F32)
+    halos = [chunk_halo(ylo[page, s], yhi[page, s], step, lane) for s in range(count)]
     for k in range(depth):
-        z = step * depth + k
         reaction = rate_const * gas[0, k] * gas[1, k]
         total = None
         for s in range(count):
@@ -188,7 +196,7 @@
             below = gas[s, k - 1] if k > 0 else jnp.where(at_bottom, zlo[s], before[s, 0])
             above = gas[s, k + 1] if k < depth - 1 else jnp.where(at_top, zhi[s], after[s, 0])
             west, east, south, north = shifted(
-                center, row, lane, z, xlo[s, k : k + 1], xhi[s, k : k + 1], ylo[s], yhi[s]
+                center, row, lane, k, xlo[s, k : k + 1], xhi[s, k : k + 1], halos[s]
             )
             beside = (below + above) + (west + east) + (south + north)
             value = (
@@ -201,12 +209,10 @@
             total = value if total is None else total + value
         mix = 0.5 * total
         mix_out[k] = mix
-        first = pack_columns(first, mix, z, lane, False)
-        last = pack_columns(last, mix, z, lane, True)
+        packed = pack_columns(packed, mix, k, lane)
         x_first[k : k + 1] = mix[0:1]
         x_last[k : k + 1] = mix[rows - 1 : rows]
-    y_first[...] = first
-    y_last[...] = last
+    y_pair[page] += pltpu.roll(packed, offset, 1)
 
 
 def lookup(flags, table):
@@ -228,6 +234,10 @@
     loss = lookup(flags[...], loss_table)
     feed = lookup(flags[...], feed_table)
     rate = exchange[...]
+    page, _ = page_of(step, lanes)
+    heat_halo = chunk_halo(ylo[page, 6], yhi[page, 6], step, lane)
+    temp_halo = chunk_halo(ylo[page, 7], yhi[page, 7], step, lane)
+    mix_halo = chunk_halo(mylo[page], myhi[page], step, lane)
     for k in range(depth):
         z = step * depth + k
         reaction = rate_const * pair[0, k] * pair[1, k]
@@ -238,12 +248,12 @@
         mix_above = mix[k + 1] if k < depth - 1 else jnp.where(at_top, mzhi[...], mix_after[0])
         one = slice(k, k + 1)
         heats = (heat_below, heat_above) + shifted(
-            heat_mid, row, lane, z, xlo[6, one], xhi[6, one], ylo[6], yhi[6]
+            heat_mid, row, lane, k, xlo[6, one], xhi[6, one], heat_halo
         )
         mixes = (mix_below, mix_above) + shifted(
-            mix_mid, row, lane, z, mxlo[one], mxhi[one], mylo[...], myhi[...]
+            mix_mid, row, lane, k, mxlo[one], mxhi[one], mix_halo
         )
-        temps = shifted(temp_mid, row, lane, z, xlo[7, one], xhi[7, one], ylo[7], yhi[7])
+        temps = shifted(temp_mid, row, lane, k, xlo[7, one], xhi[7, one], temp_halo)
         cond_mid = cond_base + cond_slope * mix_mid
         flux = None
         for heat_near, mix_near in zip(heats, mixes):
@@ -374,32 +384,34 @@
     planes = pl.BlockSpec((CHUNK, rows, lanes), lambda i: (i, 0, 0))
     edge = pl.BlockSpec((CHUNK, lanes), lambda i: (i, 0))
     edges = pl.BlockSpec((fields, CHUNK, lanes), lambda i: (0, i, 0))
-    sides = fixed(fields, rows, lanes)
+    pages = -(-2 * depth // lanes)
+    sides = fixed(pages, fields, rows, lanes)
     tops = fixed(count + 1, rows, lanes)
     side = fixed(rows, lanes)
-
-    x_first, x_last, y_first, y_last = pl.pallas_call(
+    mix_sides = fixed(pages, rows, lanes)
+
+    x_first, x_last, y_pair = pl.pallas_call(
         pack_kernel,
         grid=(steps,),
-        out_shape=[shape(fields, depth, lanes)] * 2 + [shape(fields, rows, lanes)] * 2,
+        out_shape=[shape(fields, depth, lanes)] * 2 + [shape(pages, fields, rows, lanes)],
         in_specs=[stack(count + 1, 0), planes],
-        out_specs=[edges, edges, sides, sides],
+        out_specs=[edges, edges, sides],
         compiler_params=params(),
     )(gas_state, solids_temp)
     zlo, zhi, xlo, xhi, ylo, yhi = swap(
-        gas_state, x_first, x_last, y_first, y_last, 0
+        gas_state, x_first, x_last, y_pair, 0
     )
-    gas_next, mix, mx_first, mx_last, my_first, my_last = pl.pallas_call(
+    gas_next, mix, mx_first, mx_last, my_pair = pl.pallas_call(
         species_kernel,
         grid=(steps,),
         out_shape=[shape(count + 1, depth, rows, lanes), shape(depth, rows, lanes)]
         + [shape(depth, lanes)] * 2
-        + [shape(rows, lanes)] * 2,
+        + [shape(pages, rows, lanes)],
         in_specs=[stack(count, 0), below_of(count, 0), above_of(count, 0), tops, tops, edges, edges, sides, sides],
-        out_specs=[stack(count, 0), planes, edge, edge, side, side],
+        out_specs=[stack(count, 0), planes, edge, edge, mix_sides],
         compiler_params=params(),
     )(gas_state, gas_state, gas_state, zlo, zhi, xlo, xhi, ylo, yhi)
-    mix_halos = swap(mix, mx_first, mx_last, my_first, my_last, 1)
+    mix_halos = swap(mix, mx_first, mx_last, my_pair, 1)
     mix_below = pl.BlockSpec((1, rows, lanes), lambda i: (jnp.maximum(i * CHUNK - 1, 0), 0, 0))
     mix_above = pl.BlockSpec((1, rows, lanes), lambda i: (jnp.minimum((i + 1) * CHUNK, depth - 1), 0, 0))
     gas_next, local, ends = pl.pallas_call(
@@ -415,7 +427,7 @@
             planes, mix_below, mix_above, planes, side, side,
             fixed(*block_inverse.shape), fixed(*line_coupling.shape),
             tops, tops, edges, edges, sides, sides,
-            side, side, edge, edge, side, side, ANY,
+            side, side, edge, edge, mix_sides, mix_sides, ANY,
         ],
         out_specs=[stack(1, count), fixed(depth * rows, lanes), fixed(2 * rows + 8, lanes)],
         scratch_shapes=[pltpu.VMEM((depth * rows, lanes), F32)],

time: 52.9 us -> 50.5 us (0.955)
  Pallas kernels: 51.8 us -> 49.4 us
    pallas_call x1, Pallas kernels: 14.9 us -> 12 us  [body(): pl.pallas_call(species_kernel, grid=(steps,), out_shape=[shape(count + 1,...]
where the time goes in v3:
time: 50.5 us; the launch traced here: 50 us
  Pallas kernels  49.4 us (98%)
  between operations  0.66 us (1%)
    pallas_call x2, Pallas kernels, swap(): pl.pallas_call(swap_kernel, out_shape=[top, top, side, side, edge, edge],...  13.8 us
    pallas_call x1, Pallas kernels, body(): pl.pallas_call(species_kernel, grid=(steps,), out_shape=[shape(count + 1,...  12 us
    pallas_call x1, Pallas kernels, body(): pl.pallas_call(energy_kernel, grid=(steps,), out_shape=[shape(count + 1,...  7.95 us
    pallas_call x1, Pallas kernels, body(): pl.pallas_call(pack_kernel, grid=(steps,), out_shape=[shape(fields, depth...  7.15 us
    pallas_call x1, Pallas kernels, body(): pl.pallas_call(share_kernel, out_shape=shape(segments, 2 * rows + 8, lane...  5.41 us
    pallas_call x1, Pallas kernels, body(): pl.pallas_call(finish_kernel, out_shape=shape(depth * rows, lanes), grid=...  3.09 us

profile of v3, /device:TPU:0, one launch (start us, length us, event | category | flops | bytes accessed | tf_op | source)
XLA Modules:
  0.0 50.0 jit_solution(224293784681566612)
XLA Ops:
  0.6 7.2 %shard_map.77 = (f32[8,96,128]{2,1,0:T(8,128)}, f32[8,96,128]{2,1,0:T(8,128)}, f32[2,8,16,128]{3,2,1,0:T(8,128)}) custom-call(f32[7,96,16,128]{3,2,1,0:T(8,128)} %heat_after.1, f32[96,16,128]{2,1,0:T(8,128)} %temp.3), custom_call_target="tpu_custom_call" | custom-call | tf_op jit(solution)/shard_map/pallas_call | solution.py:393
  7.8 8.4 %shard_map.78 = (f32[7,16,128]{2,1,0:T(8,128)}, f32[7,16,128]{2,1,0:T(8,128)}, f32[8,96,128]{2,1,0:T(8,128)}, f32[8,96,128]{2,1,0:T(8,128)}, f32[2,8,16,128]{3,2,1,0:T(8,128)}, /*index=5*/f32[2,8,16,128]{3,2,1,0:T(8,128)}) custom-call(f32[7,96,16,128]{3,2,1,0:T(8,128)} %heat_after.1, f32[8,96,128]{2,1,0:T(8,128)} %get-tuple-element.25.x_first, ...), custom_call_target="tpu_custom_call" | custom-call | tf_op jit(solution)/shard_map/pallas_call | solution.py:166
  16.2 12.0 %shard_map.79 = (f32[7,96,16,128]{3,2,1,0:T(8,128)}, f32[96,16,128]{2,1,0:T(8,128)}, f32[96,128]{1,0:T(8,128)}, f32[96,128]{1,0:T(8,128)}, f32[2,16,128]{2,1,0:T(8,128)}) custom-call(f32[7,96,16,128]{3,2,1,0:T(8,128)} %heat_after.1, f32[7,96,16,128]{3,2,1,0:T(8,128)} %heat_after.1, f32[7,96,16,128]{3,2,1,0:T(8,128)} %heat_after.1, ...), custom_call_target="tpu_custom_call" | custom-call | tf_op jit(solution)/shard_map/pallas_call | solution.py:404
  28.2 5.4 %shard_map.80 = (f32[16,128]{1,0:T(8,128)}, f32[16,128]{1,0:T(8,128)}, f32[96,128]{1,0:T(8,128)}, f32[96,128]{1,0:T(8,128)}, f32[2,16,128]{2,1,0:T(8,128)}, /*index=5*/f32[2,16,128]{2,1,0:T(8,128)}) custom-call(f32[96,16,128]{2,1,0:T(8,128)} %get-tuple-element.34.field.mix.mix_before.mix_after, f32[96,128]{1,0:T(8,128)} %get-tuple-element.35.x_first, ...), custom_call_target="tpu_custom_call" | custom-call | tf_op jit(solution)/shard_map/pallas_call | solution.py:166
  33.6 8.0 %shard_map.81 = (f32[7,96,16,128]{3,2,1,0:T(8,128)}, f32[1536,128]{1,0:T(8,128)}, f32[40,128]{1,0:T(8,128)}) custom-call(f32[7,96,16,128]{3,2,1,0:T(8,128)} %heat_after.1, f32[7,96,16,128]{3,2,1,0:T(8,128)} %heat_after.1, f32[7,96,16,128]{3,2,1,0:T(8,128)} %heat_after.1, f32[7,96,16,128]{3,2,1,0:T(8,128)} %heat_after.1, ...), custom_call_target="tpu_custom_call", output_to_operand_aliasing={{0}: (24, {})} | custom-call | tf_op jit(solution)/shard_map/pallas_call | solution.py:417
  41.5 5.4 %shard_map.82.slots = f32[4,40,128]{2,1,0:T(8,128)} custom-call(f32[40,128]{1,0:T(8,128)} %get-tuple-element.46.ends), custom_call_target="tpu_custom_call" | custom-call | tf_op jit(solution)/shard_map/pallas_call | solution.py:440
  46.9 3.1 %shard_map.83 = f32[1536,128]{1,0:T(8,128)} custom-call(f32[4,40,128]{2,1,0:T(8,128)} %shard_map.82.slots, f32[1536,128]{1,0:T(8,128)} %get-tuple-element.47.local, f32[96,96]{1,0:T(8,128)} %inverse.3), custom_call_target="tpu_custom_call" | custom-call | tf_op jit(solution)/shard_map/pallas_call | solution.py:449

commit v4 on v3

--- a/solution.py
+++ b/solution.py
@@ -71,28 +71,87 @@
     return west, east, south, north
 
 
-def pack_kernel(gas, temp, x_first, x_last, y_pair):
-    step = pl.program_id(0)
+def pack_field(read, field, chunk, x_first, x_last, y_pair):
+    rows, lanes = y_pair.shape[2:]
+    _, lane = iotas(rows, lanes)
+    packed = jnp.zeros((rows, lanes), F32)
+    for k in range(CHUNK):
+        z = chunk * CHUNK + k
+        plane = read(z)
+        packed = pack_columns(packed, plane, k, lane)
+        x_first[field, z : z + 1] = plane[0:1]
+        x_last[field, z : z + 1] = plane[rows - 1 : rows]
+    per_page = lanes // (2 * CHUNK)
+    page, offset = chunk // per_page, chunk % per_page * (2 * CHUNK)
+    moved = pltpu.roll(packed, offset, 1) if offset else packed
+    y_pair[page, field] = moved if offset == 0 else y_pair[page, field] + moved
+
+
+def pack_swap_kernel(
+    gas, temp, zlo, zhi, xlo, xhi, ylo, yhi,
+    gas_held, temp_held, x_first, x_last, y_pair, x_blank, z_blank, y_blank, load_sem, zero_sem, send_sem, recv_sem,
+):
+    fields, depth = gas.shape[:2]
+    loads = []
+    for chunk in range(depth // CHUNK):
+        span = pl.ds(chunk * CHUNK, CHUNK)
+        loads.append(
+            (
+                pltpu.make_async_copy(gas.at[:, span], gas_held.at[:, span], load_sem.at[2 * chunk]),
+                pltpu.make_async_copy(temp.at[span], temp_held.at[span], load_sem.at[2 * chunk + 1]),
+            )
+        )
+    for pair in loads:
+        for load in pair:
+            load.start()
+
+    def prepare():
+        for chunk, pair in enumerate(loads):
+            for load in pair:
+                load.wait()
+
+            def one(field, carry, chunk=chunk):
+                pack_field(lambda z: gas_held[field, z], field, chunk, x_first, x_last, y_pair)
+                return carry
+
+            lax.fori_loop(0, fields, one, 0)
+            pack_field(lambda z: temp_held[z], fields, chunk, x_first, x_last, y_pair)
+
+    swap_faces(
+        (
+            ("gx", x_first, x_last, xlo, xhi),
+            ("seg", gas.at[:, 0], gas.at[:, depth - 1], zlo, zhi),
+            ("gy", y_pair, y_pair, ylo, yhi),
+        ),
+        (x_blank, z_blank, y_blank),
+        zero_sem,
+        send_sem,
+        recv_sem,
+        prepare,
+    )
+
+
+def pack_swap(gas, temp, pages, ident):
     fields = gas.shape[0] + 1
-    rows, lanes = gas.shape[2:]
-    _, lane = iotas(rows, lanes)
-
-    @pl.when(step == 0)
-    def _():
-        y_pair[...] = jnp.zeros_like(y_pair)
-
-    page, offset = page_of(step, lanes)
-    for field in range(fields):
-        packed = jnp.zeros((rows, lanes), F32)
-        for k in range(gas.shape[1]):
-            plane = gas[field, k] if field < fields - 1 else temp[k]
-            packed = pack_columns(packed, plane, k, lane)
-            x_first[field, k : k + 1] = plane[0:1]
-            x_last[field, k : k + 1] = plane[rows - 1 : rows]
-        y_pair[page, field] += pltpu.roll(packed, offset, 1)
-
-
-def swap_faces(axes, blanks, zero_sem, send_sem, recv_sem):
+    depth, rows, lanes = temp.shape
+    top = shape(gas.shape[0], rows, lanes)
+    side = shape(fields, depth, lanes)
+    edge = shape(pages, fields, rows, lanes)
+    sems = pltpu.SemaphoreType.DMA((6,))
+    return pl.pallas_call(
+        pack_swap_kernel,
+        out_shape=[top, top, side, side, edge, edge],
+        in_specs=[ANY] * 2,
+        out_specs=[ANY] * 6,
+        scratch_shapes=[
+            pltpu.VMEM(held.shape, F32) for held in (gas, temp, side, side, edge, side, top, edge)
+        ]
+        + [pltpu.SemaphoreType.DMA((2 * (depth // CHUNK),)), sems, sems, sems],
+        compiler_params=pltpu.CompilerParams(collective_id=ident, has_side_effects=True, vmem_limit_bytes=63 * 1024 * 1024),
+    )(gas, temp)
+
+
+def swap_faces(axes, blanks, zero_sem, send_sem, recv_sem, prepare=None):
     barrier = pltpu.get_barrier_semaphore()
     places = []
     for name, *_ in axes:
@@ -117,7 +176,8 @@
             src_ref=first, dst_ref=high, send_sem=send_sem.at[2 * index + 1], recv_sem=recv_sem.at[2 * index + 1],
             device_id={name: here - 1}, device_id_type=MESH)
         plan.append((to_up, to_down, down, up, low, high))
-    for to_up, to_down, down, up, low, high in plan:
+    early = [entry for entry, axis in zip(plan, axes) if prepare is None or axis[0] == "seg"]
+    for to_up, to_down, down, up, _, _ in early:
         pl.when(up)(to_up.start)
         pl.when(down)(to_down.start)
     for blank in blanks:
@@ -129,6 +189,12 @@
             fills.append((jnp.logical_not(exists), fill))
     for missing, fill in fills:
         pl.when(missing)(fill.start)
+    if prepare is not None:
+        prepare()
+        for (to_up, to_down, down, up, _, _), axis in zip(plan, axes):
+            if axis[0] != "seg":
+                pl.when(up)(to_up.start)
+                pl.when(down)(to_down.start)
     for to_up, to_down, down, up, low, high in plan:
         pl.when(up)(to_up.wait_send)
         pl.when(down)(to_down.wait_send)
@@ -390,17 +456,7 @@
     side = fixed(rows, lanes)
     mix_sides = fixed(pages, rows, lanes)
 
-    x_first, x_last, y_pair = pl.pallas_call(
-        pack_kernel,
-        grid=(steps,),
-        out_shape=[shape(fields, depth, lanes)] * 2 + [shape(pages, fields, rows, lanes)],
-        in_specs=[stack(count + 1, 0), planes],
-        out_specs=[edges, edges, sides],
-        compiler_params=params(),
-    )(gas_state, solids_temp)
-    zlo, zhi, xlo, xhi, ylo, yhi = swap(
-        gas_state, x_first, x_last, y_pair, 0
-    )
+    zlo, zhi, xlo, xhi, ylo, yhi = pack_swap(gas_state, solids_temp, pages, 0)
     gas_next, mix, mx_first, mx_last, my_pair = pl.pallas_call(
         species_kernel,
         grid=(steps,),

time: 50.5 us -> 49.9 us (0.988)
    pallas_call x2 -> x1, Pallas kernels: 13.8 us -> 5.36 us  [swap(): pl.pallas_call(swap_kernel, out_shape=[top, top, side, side, edge, edge],...]
    pallas_call x1, Pallas kernels: 7.15 us -> 15.1 us  [pack_swap(): pl.pallas_call(pack_swap_kernel, out_shape=[top, top, side, side, edge, e...]
where the time goes in v4:
time: 49.9 us; the launch traced here: 49.5 us
  Pallas kernels  48.9 us (98%)
  between operations  0.66 us (1%)
    pallas_call x1, Pallas kernels, pack_swap(): pl.pallas_call(pack_swap_kernel, out_shape=[top, top, side, side, edge, e...  15.1 us
    pallas_call x1, Pallas kernels, body(): pl.pallas_call(species_kernel, grid=(steps,), out_shape=[shape(count + 1,...  12 us
    pallas_call x1, Pallas kernels, body(): pl.pallas_call(energy_kernel, grid=(steps,), out_shape=[shape(count + 1,...  7.95 us
    pallas_call x1, Pallas kernels, body(): pl.pallas_call(share_kernel, out_shape=shape(segments, 2 * rows + 8, lane...  5.41 us
    pallas_call x1, Pallas kernels, swap(): pl.pallas_call(swap_kernel, out_shape=[top, top, side, side, edge, edge],...  5.36 us
    pallas_call x1, Pallas kernels, body(): pl.pallas_call(finish_kernel, out_shape=shape(depth * rows, lanes), grid=...  3.09 us

profile of v4, /device:TPU:0, one launch (start us, length us, event | category | flops | bytes accessed | tf_op | source)
XLA Modules:
  0.0 49.5 jit_solution(10938620218304470126)
XLA Ops:
  0.6 15.1 %shard_map.77 = (f32[7,16,128]{2,1,0:T(8,128)}, f32[7,16,128]{2,1,0:T(8,128)}, f32[8,96,128]{2,1,0:T(8,128)}, f32[8,96,128]{2,1,0:T(8,128)}, f32[2,8,16,128]{3,2,1,0:T(8,128)}, /*index=5*/f32[2,8,16,128]{3,2,1,0:T(8,128)}) custom-call(f32[7,96,16,128]{3,2,1,0:T(8,128)} %heat_after.1, f32[96,16,128]{2,1,0:T(8,128)} %temp.3), custom_call_target="tpu_custom_call" | custom-call | tf_op jit(solution)/shard_map/pallas_call | solution.py:141
  15.7 12.0 %shard_map.78 = (f32[7,96,16,128]{3,2,1,0:T(8,128)}, f32[96,16,128]{2,1,0:T(8,128)}, f32[96,128]{1,0:T(8,128)}, f32[96,128]{1,0:T(8,128)}, f32[2,16,128]{2,1,0:T(8,128)}) custom-call(f32[7,96,16,128]{3,2,1,0:T(8,128)} %heat_after.1, f32[7,96,16,128]{3,2,1,0:T(8,128)} %heat_after.1, f32[7,96,16,128]{3,2,1,0:T(8,128)} %heat_after.1, ...), custom_call_target="tpu_custom_call" | custom-call | tf_op jit(solution)/shard_map/pallas_call | solution.py:460
  27.7 5.4 %shard_map.79 = (f32[16,128]{1,0:T(8,128)}, f32[16,128]{1,0:T(8,128)}, f32[96,128]{1,0:T(8,128)}, f32[96,128]{1,0:T(8,128)}, f32[2,16,128]{2,1,0:T(8,128)}, /*index=5*/f32[2,16,128]{2,1,0:T(8,128)}) custom-call(f32[96,16,128]{2,1,0:T(8,128)} %get-tuple-element.28.field.mix.mix_before.mix_after, f32[96,128]{1,0:T(8,128)} %get-tuple-element.29.x_first, ...), custom_call_target="tpu_custom_call" | custom-call | tf_op jit(solution)/shard_map/pallas_call | solution.py:232
  33.1 7.9 %shard_map.80 = (f32[7,96,16,128]{3,2,1,0:T(8,128)}, f32[1536,128]{1,0:T(8,128)}, f32[40,128]{1,0:T(8,128)}) custom-call(f32[7,96,16,128]{3,2,1,0:T(8,128)} %heat_after.1, f32[7,96,16,128]{3,2,1,0:T(8,128)} %heat_after.1, f32[7,96,16,128]{3,2,1,0:T(8,128)} %heat_after.1, f32[7,96,16,128]{3,2,1,0:T(8,128)} %heat_after.1, ...), custom_call_target="tpu_custom_call", output_to_operand_aliasing={{0}: (24, {})} | custom-call | tf_op jit(solution)/shard_map/pallas_call | solution.py:473
  41.0 5.4 %shard_map.81.slots = f32[4,40,128]{2,1,0:T(8,128)} custom-call(f32[40,128]{1,0:T(8,128)} %get-tuple-element.40.ends), custom_call_target="tpu_custom_call" | custom-call | tf_op jit(solution)/shard_map/pallas_call | solution.py:496
  46.5 3.1 %shard_map.82 = f32[1536,128]{1,0:T(8,128)} custom-call(f32[4,40,128]{2,1,0:T(8,128)} %shard_map.81.slots, f32[1536,128]{1,0:T(8,128)} %get-tuple-element.41.local, f32[96,96]{1,0:T(8,128)} %inverse.3), custom_call_target="tpu_custom_call" | custom-call | tf_op jit(solution)/shard_map/pallas_call | solution.py:505

commit v5 on v4

--- a/solution.py
+++ b/solution.py
@@ -61,26 +61,28 @@
     return pltpu.roll(merge_pages(low, high, lane), lax.rem(lanes - offset, lanes), 1)
 
 
-def shifted(plane, row, lane, k, xlo, xhi, halo):
+def shifted(plane, row, lane, k, xlo, xhi, halo, less=None, more=None):
     rows, lanes = plane.shape
-    west = jnp.where(row == 0, xlo, pltpu.roll(plane, 1, 0))
-    east = jnp.where(row == rows - 1, xhi, pltpu.roll(plane, rows - 1, 0))
+    less = pltpu.roll(plane, 1, 0) if less is None else less
+    more = pltpu.roll(plane, rows - 1, 0) if more is None else more
+    west = jnp.where(row == 0, xlo, less)
+    east = jnp.where(row == rows - 1, xhi, more)
     column = pltpu.roll(halo, lanes - 2 * k, 1) if k else halo
     south = jnp.where(lane == 0, column, pltpu.roll(plane, 1, 1))
     north = jnp.where(lane == lanes - 1, column, pltpu.roll(plane, lanes - 1, 1))
     return west, east, south, north
 
 
-def pack_field(read, field, chunk, x_first, x_last, y_pair):
+def pack_field(held, field, chunk, x_first, x_last, y_pair):
     rows, lanes = y_pair.shape[2:]
     _, lane = iotas(rows, lanes)
     packed = jnp.zeros((rows, lanes), F32)
     for k in range(CHUNK):
         z = chunk * CHUNK + k
-        plane = read(z)
-        packed = pack_columns(packed, plane, k, lane)
-        x_first[field, z : z + 1] = plane[0:1]
-        x_last[field, z : z + 1] = plane[rows - 1 : rows]
+        packed = pack_columns(packed, held[pl.ds(z * rows, rows), :], k, lane)
+    start, span = chunk * CHUNK, pl.ds(chunk * CHUNK, CHUNK)
+    x_first[field, span] = held[pl.ds(start * rows, CHUNK, stride=rows), :]
+    x_last[field, span] = held[pl.ds(start * rows + rows - 1, CHUNK, stride=rows), :]
     per_page = lanes // (2 * CHUNK)
     page, offset = chunk // per_page, chunk % per_page * (2 * CHUNK)
     moved = pltpu.roll(packed, offset, 1) if offset else packed
@@ -91,10 +93,10 @@
     gas, temp, zlo, zhi, xlo, xhi, ylo, yhi,
     gas_held, temp_held, x_first, x_last, y_pair, x_blank, z_blank, y_blank, load_sem, zero_sem, send_sem, recv_sem,
 ):
-    fields, depth = gas.shape[:2]
+    fields, depth, rows = gas.shape[0], x_first.shape[1], y_pair.shape[2]
     loads = []
     for chunk in range(depth // CHUNK):
-        span = pl.ds(chunk * CHUNK, CHUNK)
+        span = pl.ds(chunk * CHUNK * rows, CHUNK * rows)
         loads.append(
             (
                 pltpu.make_async_copy(gas.at[:, span], gas_held.at[:, span], load_sem.at[2 * chunk]),
@@ -111,16 +113,16 @@
                 load.wait()
 
             def one(field, carry, chunk=chunk):
-                pack_field(lambda z: gas_held[field, z], field, chunk, x_first, x_last, y_pair)
+                pack_field(gas_held.at[field], field, chunk, x_first, x_last, y_pair)
                 return carry
 
             lax.fori_loop(0, fields, one, 0)
-            pack_field(lambda z: temp_held[z], fields, chunk, x_first, x_last, y_pair)
+            pack_field(temp_held, fields, chunk, x_first, x_last, y_pair)
 
     swap_faces(
         (
             ("gx", x_first, x_last, xlo, xhi),
-            ("seg", gas.at[:, 0], gas.at[:, depth - 1], zlo, zhi),
+            ("seg", gas.at[:, pl.ds(0, rows)], gas.at[:, pl.ds((depth - 1) * rows, rows)], zlo, zhi),
             ("gy", y_pair, y_pair, ylo, yhi),
         ),
         (x_blank, z_blank, y_blank),
@@ -138,17 +140,19 @@
     side = shape(fields, depth, lanes)
     edge = shape(pages, fields, rows, lanes)
     sems = pltpu.SemaphoreType.DMA((6,))
+    flat_gas = gas.reshape(gas.shape[0], depth * rows, lanes)
+    flat_temp = temp.reshape(depth * rows, lanes)
     return pl.pallas_call(
         pack_swap_kernel,
         out_shape=[top, top, side, side, edge, edge],
         in_specs=[ANY] * 2,
         out_specs=[ANY] * 6,
         scratch_shapes=[
-            pltpu.VMEM(held.shape, F32) for held in (gas, temp, side, side, edge, side, top, edge)
+            pltpu.VMEM(held.shape, F32) for held in (flat_gas, flat_temp, side, side, edge, side, top, edge)
         ]
         + [pltpu.SemaphoreType.DMA((2 * (depth // CHUNK),)), sems, sems, sems],
         compiler_params=pltpu.CompilerParams(collective_id=ident, has_side_effects=True, vmem_limit_bytes=63 * 1024 * 1024),
-    )(gas, temp)
+    )(flat_gas, flat_temp)
 
 
 def swap_faces(axes, blanks, zero_sem, send_sem, recv_sem, prepare=None):
@@ -243,7 +247,7 @@
     gas, before, after, zlo, zhi, xlo, xhi, ylo, yhi, new, mix_out, x_first, x_last, y_pair
 ):
     step, steps = pl.program_id(0), pl.num_programs(0)
-    count, depth, rows, lanes = gas.shape
+    count, depth, rows, lanes = new.shape
     row, lane = iotas(rows, lanes)
     at_bottom, at_top = step == 0, step == steps - 1
 
@@ -255,14 +259,18 @@
     packed = jnp.zeros((rows, lanes), F32)
     halos = [chunk_halo(ylo[page, s], yhi[page, s], step, lane) for s in range(count)]
     for k in range(depth):
-        reaction = rate_const * gas[0, k] * gas[1, k]
+        here = slice(k * rows, (k + 1) * rows)
+        reaction = rate_const * gas[0, here] * gas[1, here]
         total = None
         for s in range(count):
-            center = gas[s, k]
-            below = gas[s, k - 1] if k > 0 else jnp.where(at_bottom, zlo[s], before[s, 0])
-            above = gas[s, k + 1] if k < depth - 1 else jnp.where(at_top, zhi[s], after[s, 0])
+            center = gas[s, here]
+            down, up = slice((k - 1) * rows, k * rows), slice((k + 1) * rows, (k + 2) * rows)
+            below = gas[s, down] if k > 0 else jnp.where(at_bottom, zlo[s], before[s])
+            above = gas[s, up] if k < depth - 1 else jnp.where(at_top, zhi[s], after[s])
+            less = gas[s, k * rows - 1 : (k + 1) * rows - 1] if k > 0 else None
+            more = gas[s, k * rows + 1 : (k + 1) * rows + 1] if k < depth - 1 else None
             west, east, south, north = shifted(
-                center, row, lane, k, xlo[s, k : k + 1], xhi[s, k : k + 1], halos[s]
+                center, row, lane, k, xlo[s, k : k + 1], xhi[s, k : k + 1], halos[s], less, more
             )
             beside = (below + above) + (west + east) + (south + north)
             value = (
@@ -457,16 +465,21 @@
     mix_sides = fixed(pages, rows, lanes)
 
     zlo, zhi, xlo, xhi, ylo, yhi = pack_swap(gas_state, solids_temp, pages, 0)
+    flat = gas_state.reshape(count + 1, depth * rows, lanes)
     gas_next, mix, mx_first, mx_last, my_pair = pl.pallas_call(
         species_kernel,
         grid=(steps,),
         out_shape=[shape(count + 1, depth, rows, lanes), shape(depth, rows, lanes)]
         + [shape(depth, lanes)] * 2
         + [shape(pages, rows, lanes)],
-        in_specs=[stack(count, 0), below_of(count, 0), above_of(count, 0), tops, tops, edges, edges, sides, sides],
+        in_specs=[
+            pl.BlockSpec((count, CHUNK * rows, lanes), lambda i: (0, i, 0)),
+            pl.BlockSpec((count, rows, lanes), lambda i: (0, jnp.maximum(i * CHUNK - 1, 0), 0)),
+            pl.BlockSpec((count, rows, lanes), lambda i: (0, jnp.minimum((i + 1) * CHUNK, depth - 1), 0)),
+            tops, tops, edges, edges, sides, sides],
         out_specs=[stack(count, 0), planes, edge, edge, mix_sides],
         compiler_params=params(),
-    )(gas_state, gas_state, gas_state, zlo, zhi, xlo, xhi, ylo, yhi)
+    )(flat, flat, flat, zlo, zhi, xlo, xhi, ylo, yhi)
     mix_halos = swap(mix, mx_first, mx_last, my_pair, 1)
     mix_below = pl.BlockSpec((1, rows, lanes), lambda i: (jnp.maximum(i * CHUNK - 1, 0), 0, 0))
     mix_above = pl.BlockSpec((1, rows, lanes), lambda i: (jnp.minimum((i + 1) * CHUNK, depth - 1), 0, 0))

time: 49.9 us -> 49.8 us (level)
  no operation moved by 1% of the time
where the time goes in v5:
time: 49.8 us; the launch traced here: 49.5 us
  Pallas kernels  48.9 us (98%)
  between operations  0.66 us (1%)
    pallas_call x1, Pallas kernels, pack_swap(): pl.pallas_call(pack_swap_kernel, out_shape=[top, top, side, side, edge, e...  15.1 us
    pallas_call x1, Pallas kernels, body(): pl.pallas_call(species_kernel, grid=(steps,), out_shape=[shape(count + 1,...  12 us
    pallas_call x1, Pallas kernels, body(): pl.pallas_call(energy_kernel, grid=(steps,), out_shape=[shape(count + 1,...  7.94 us
    pallas_call x1, Pallas kernels, body(): pl.pallas_call(share_kernel, out_shape=shape(segments, 2 * rows + 8, lane...  5.41 us
    pallas_call x1, Pallas kernels, swap(): pl.pallas_call(swap_kernel, out_shape=[top, top, side, side, edge, edge],...  5.36 us
    pallas_call x1, Pallas kernels, body(): pl.pallas_call(finish_kernel, out_shape=shape(depth * rows, lanes), grid=...  3.09 us

profile of v5, /device:TPU:0, one launch (start us, length us, event | category | flops | bytes accessed | tf_op | source)
XLA Modules:
  0.0 49.5 jit_solution(9483584154126275448)
XLA Ops:
  0.6 15.1 %shard_map.77 = (f32[7,16,128]{2,1,0:T(8,128)}, f32[7,16,128]{2,1,0:T(8,128)}, f32[8,96,128]{2,1,0:T(8,128)}, f32[8,96,128]{2,1,0:T(8,128)}, f32[2,8,16,128]{3,2,1,0:T(8,128)}, /*index=5*/f32[2,8,16,128]{3,2,1,0:T(8,128)}) custom-call(f32[7,1536,128]{2,1,0:T(8,128)} %bitcast.3, f32[1536,128]{1,0:T(8,128)} %bitcast.7), custom_call_target="tpu_custom_call" | custom-call | tf_op jit(solution)/shard_map/pallas_call | solution.py:145
  15.7 12.0 %shard_map.78 = (f32[7,96,16,128]{3,2,1,0:T(8,128)}, f32[96,16,128]{2,1,0:T(8,128)}, f32[96,128]{1,0:T(8,128)}, f32[96,128]{1,0:T(8,128)}, f32[2,16,128]{2,1,0:T(8,128)}) custom-call(f32[7,1536,128]{2,1,0:T(8,128)} %bitcast.4, f32[7,1536,128]{2,1,0:T(8,128)} %bitcast.5, f32[7,1536,128]{2,1,0:T(8,128)} %bitcast.6, f32[7,16,128]{2,1,0:T(8,128)} %get-tuple-element.22.zlo, ...), custom_call_target="tpu_custom_call" | custom-call | tf_op jit(solution)/shard_map/pallas_call | solution.py:469
  27.7 5.4 %shard_map.79 = (f32[16,128]{1,0:T(8,128)}, f32[16,128]{1,0:T(8,128)}, f32[96,128]{1,0:T(8,128)}, f32[96,128]{1,0:T(8,128)}, f32[2,16,128]{2,1,0:T(8,128)}, /*index=5*/f32[2,16,128]{2,1,0:T(8,128)}) custom-call(f32[96,16,128]{2,1,0:T(8,128)} %get-tuple-element.28.field.mix.mix_before.mix_after, f32[96,128]{1,0:T(8,128)} %get-tuple-element.29.x_first, ...), custom_call_target="tpu_custom_call" | custom-call | tf_op jit(solution)/shard_map/pallas_call | solution.py:236
  33.1 7.9 %shard_map.80 = (f32[7,96,16,128]{3,2,1,0:T(8,128)}, f32[1536,128]{1,0:T(8,128)}, f32[40,128]{1,0:T(8,128)}) custom-call(f32[7,96,16,128]{3,2,1,0:T(8,128)} %heat_after.1, f32[7,96,16,128]{3,2,1,0:T(8,128)} %heat_after.1, f32[7,96,16,128]{3,2,1,0:T(8,128)} %heat_after.1, f32[7,96,16,128]{3,2,1,0:T(8,128)} %heat_after.1, ...), custom_call_target="tpu_custom_call", output_to_operand_aliasing={{0}: (24, {})} | custom-call | tf_op jit(solution)/shard_map/pallas_call | solution.py:486
  41.0 5.4 %shard_map.81.slots = f32[4,40,128]{2,1,0:T(8,128)} custom-call(f32[40,128]{1,0:T(8,128)} %get-tuple-element.40.ends), custom_call_target="tpu_custom_call" | custom-call | tf_op jit(solution)/shard_map/pallas_call | solution.py:509
  46.4 3.1 %shard_map.82 = f32[1536,128]{1,0:T(8,128)} custom-call(f32[4,40,128]{2,1,0:T(8,128)} %shard_map.81.slots, f32[1536,128]{1,0:T(8,128)} %get-tuple-element.41.local, f32[96,96]{1,0:T(8,128)} %inverse.3), custom_call_target="tpu_custom_call" | custom-call | tf_op jit(solution)/shard_map/pallas_call | solution.py:518

commit v6 on v5

--- a/solution.py
+++ b/solution.py
@@ -309,25 +309,25 @@
     feed = lookup(flags[...], feed_table)
     rate = exchange[...]
     page, _ = page_of(step, lanes)
-    heat_halo = chunk_halo(ylo[page, 6], yhi[page, 6], step, lane)
-    temp_halo = chunk_halo(ylo[page, 7], yhi[page, 7], step, lane)
+    heat_halo = chunk_halo(ylo[page, 0], yhi[page, 0], step, lane)
+    temp_halo = chunk_halo(ylo[page, 1], yhi[page, 1], step, lane)
     mix_halo = chunk_halo(mylo[page], myhi[page], step, lane)
     for k in range(depth):
         z = step * depth + k
         reaction = rate_const * pair[0, k] * pair[1, k]
         heat_mid, mix_mid, temp_mid = heat[0, k], mix[k], temp[k]
-        heat_below = heat[0, k - 1] if k > 0 else jnp.where(at_bottom, zlo[6], heat_before[0, 0])
-        heat_above = heat[0, k + 1] if k < depth - 1 else jnp.where(at_top, zhi[6], heat_after[0, 0])
+        heat_below = heat[0, k - 1] if k > 0 else jnp.where(at_bottom, zlo[0], heat_before[0, 0])
+        heat_above = heat[0, k + 1] if k < depth - 1 else jnp.where(at_top, zhi[0], heat_after[0, 0])
         mix_below = mix[k - 1] if k > 0 else jnp.where(at_bottom, mzlo[...], mix_before[0])
         mix_above = mix[k + 1] if k < depth - 1 else jnp.where(at_top, mzhi[...], mix_after[0])
         one = slice(k, k + 1)
         heats = (heat_below, heat_above) + shifted(
-            heat_mid, row, lane, k, xlo[6, one], xhi[6, one], heat_halo
+            heat_mid, row, lane, k, xlo[0, one], xhi[0, one], heat_halo
         )
         mixes = (mix_below, mix_above) + shifted(
             mix_mid, row, lane, k, mxlo[one], mxhi[one], mix_halo
         )
-        temps = shifted(temp_mid, row, lane, k, xlo[7, one], xhi[7, one], temp_halo)
+        temps = shifted(temp_mid, row, lane, k, xlo[1, one], xhi[1, one], temp_halo)
         cond_mid = cond_base + cond_slope * mix_mid
         flux = None
         for heat_near, mix_near in zip(heats, mixes):
@@ -439,7 +439,6 @@
     depth, rows, lanes = solids_temp.shape
     segments = lax.axis_size("seg")
     steps = depth // CHUNK
-    fields = count + 2
 
     def fixed(*dims):
         return pl.BlockSpec(dims, lambda i: (0,) * len(dims))
@@ -457,10 +456,13 @@
 
     planes = pl.BlockSpec((CHUNK, rows, lanes), lambda i: (i, 0, 0))
     edge = pl.BlockSpec((CHUNK, lanes), lambda i: (i, 0))
-    edges = pl.BlockSpec((fields, CHUNK, lanes), lambda i: (0, i, 0))
+    edges = pl.BlockSpec((count, CHUNK, lanes), lambda i: (0, i, 0))
+    last_edges = pl.BlockSpec((2, CHUNK, lanes), lambda i: (count // 2, i, 0))
+    last_top = pl.BlockSpec((1, rows, lanes), lambda i: (count, 0, 0))
     pages = -(-2 * depth // lanes)
-    sides = fixed(pages, fields, rows, lanes)
-    tops = fixed(count + 1, rows, lanes)
+    sides = fixed(pages, count, rows, lanes)
+    last_sides = pl.BlockSpec((pages, 2, rows, lanes), lambda i: (0, count // 2, 0, 0))
+    tops = fixed(count, rows, lanes)
     side = fixed(rows, lanes)
     mix_sides = fixed(pages, rows, lanes)
 
@@ -495,7 +497,7 @@
             stack(2, 0), stack(1, count), below_of(1, count), above_of(1, count),
             planes, mix_below, mix_above, planes, side, side,
             fixed(*block_inverse.shape), fixed(*line_coupling.shape),
-            tops, tops, edges, edges, sides, sides,
+            last_top, last_top, last_edges, last_edges, last_sides, last_sides,
             side, side, edge, edge, mix_sides, mix_sides, ANY,
         ],
         out_specs=[stack(1, count), fixed(depth * rows, lanes), fixed(2 * rows + 8, lanes)],

time: 49.8 us -> 49.6 us (level)
  no operation moved by 1% of the time
where the time goes in v6:
time: 49.6 us; the launch traced here: 49.3 us
  Pallas kernels  48.7 us (98%)
  between operations  0.66 us (1%)
    pallas_call x1, Pallas kernels, pack_swap(): pl.pallas_call(pack_swap_kernel, out_shape=[top, top, side, side, edge, e...  15.1 us
    pallas_call x1, Pallas kernels, body(): pl.pallas_call(species_kernel, grid=(steps,), out_shape=[shape(count + 1,...  12 us
    pallas_call x1, Pallas kernels, body(): pl.pallas_call(energy_kernel, grid=(steps,), out_shape=[shape(count + 1,...  7.74 us
    pallas_call x1, Pallas kernels, body(): pl.pallas_call(share_kernel, out_shape=shape(segments, 2 * rows + 8, lane...  5.41 us
    pallas_call x1, Pallas kernels, swap(): pl.pallas_call(swap_kernel, out_shape=[top, top, side, side, edge, edge],...  5.36 us
    pallas_call x1, Pallas kernels, body(): pl.pallas_call(finish_kernel, out_shape=shape(depth * rows, lanes), grid=...  3.09 us

profile of v6, /device:TPU:0, one launch (start us, length us, event | category | flops | bytes accessed | tf_op | source)
XLA Modules:
  0.0 49.3 jit_solution(9512058172211187460)
XLA Ops:
  0.6 15.1 %shard_map.77 = (f32[7,16,128]{2,1,0:T(8,128)}, f32[7,16,128]{2,1,0:T(8,128)}, f32[8,96,128]{2,1,0:T(8,128)}, f32[8,96,128]{2,1,0:T(8,128)}, f32[2,8,16,128]{3,2,1,0:T(8,128)}, /*index=5*/f32[2,8,16,128]{3,2,1,0:T(8,128)}) custom-call(f32[7,1536,128]{2,1,0:T(8,128)} %bitcast.3, f32[1536,128]{1,0:T(8,128)} %bitcast.7), custom_call_target="tpu_custom_call" | custom-call | tf_op jit(solution)/shard_map/pallas_call | solution.py:145
  15.7 12.0 %shard_map.78 = (f32[7,96,16,128]{3,2,1,0:T(8,128)}, f32[96,16,128]{2,1,0:T(8,128)}, f32[96,128]{1,0:T(8,128)}, f32[96,128]{1,0:T(8,128)}, f32[2,16,128]{2,1,0:T(8,128)}) custom-call(f32[7,1536,128]{2,1,0:T(8,128)} %bitcast.4, f32[7,1536,128]{2,1,0:T(8,128)} %bitcast.5, f32[7,1536,128]{2,1,0:T(8,128)} %bitcast.6, f32[7,16,128]{2,1,0:T(8,128)} %get-tuple-element.22.zlo, ...), custom_call_target="tpu_custom_call" | custom-call | tf_op jit(solution)/shard_map/pallas_call | solution.py:471
  27.7 5.4 %shard_map.79 = (f32[16,128]{1,0:T(8,128)}, f32[16,128]{1,0:T(8,128)}, f32[96,128]{1,0:T(8,128)}, f32[96,128]{1,0:T(8,128)}, f32[2,16,128]{2,1,0:T(8,128)}, /*index=5*/f32[2,16,128]{2,1,0:T(8,128)}) custom-call(f32[96,16,128]{2,1,0:T(8,128)} %get-tuple-element.28.field.mix.mix_before.mix_after, f32[96,128]{1,0:T(8,128)} %get-tuple-element.29.x_first, ...), custom_call_target="tpu_custom_call" | custom-call | tf_op jit(solution)/shard_map/pallas_call | solution.py:236
  33.1 7.7 %shard_map.80 = (f32[7,96,16,128]{3,2,1,0:T(8,128)}, f32[1536,128]{1,0:T(8,128)}, f32[40,128]{1,0:T(8,128)}) custom-call(f32[7,96,16,128]{3,2,1,0:T(8,128)} %heat_after.1, f32[7,96,16,128]{3,2,1,0:T(8,128)} %heat_after.1, f32[7,96,16,128]{3,2,1,0:T(8,128)} %heat_after.1, f32[7,96,16,128]{3,2,1,0:T(8,128)} %heat_after.1, ...), custom_call_target="tpu_custom_call", output_to_operand_aliasing={{0}: (24, {})} | custom-call | tf_op jit(solution)/shard_map/pallas_call | solution.py:488
  40.8 5.4 %shard_map.81.slots = f32[4,40,128]{2,1,0:T(8,128)} custom-call(f32[40,128]{1,0:T(8,128)} %get-tuple-element.40.ends), custom_call_target="tpu_custom_call" | custom-call | tf_op jit(solution)/shard_map/pallas_call | solution.py:511
  46.2 3.1 %shard_map.82 = f32[1536,128]{1,0:T(8,128)} custom-call(f32[4,40,128]{2,1,0:T(8,128)} %shard_map.81.slots, f32[1536,128]{1,0:T(8,128)} %get-tuple-element.41.local, f32[96,96]{1,0:T(8,128)} %inverse.3), custom_call_target="tpu_custom_call" | custom-call | tf_op jit(solution)/shard_map/pallas_call | solution.py:520
